TPU v7x, 128 devices: a whole 4x4x4 slice. The times are simulated.
128 devices in a mesh: shard: 32 (over x, z, core), tensor: 4 (over y).
Axes of the slice: x: 4, y: 4, z: 4, core: 2. Of those that a mesh axis runs over, the one named last changes fastest.
Arguments:
- gradients: bfloat16 [32, 1152, 1152], P(None, 'shard', 'tensor')
- weights: float32 [32, 1152, 1152], P(None, 'shard', 'tensor'), may hold values from -0.1875 to 0.1875
- owner_list: int32 [32], replicated, may hold values from 0 to 31, as said below
- left_gram_stats: float32 [64, 1152, 1152], P('shard', 'tensor'), may hold values from -6 to 6
- right_gram_stats: float32 [64, 1152, 1152], P('shard', 'tensor'), may hold values from -6 to 6
- left_root: bfloat16 [64, 1152, 1152], P('shard', None, 'tensor'), as said below
- right_root: bfloat16 [64, 1152, 1152], P('shard', None, 'tensor'), as said below
- adam_second_moment: float32 [64, 1152, 1152], P('shard', None, 'tensor'), may hold values from 0.1 to 10
Outputs:
- new_weights: float32 [32, 1152, 1152], P(None, 'shard', 'tensor')
- new_left: float32 [64, 1152, 1152], P('shard', 'tensor')
- new_right: float32 [64, 1152, 1152], P('shard', 'tensor')
- new_moment: float32 [64, 1152, 1152], P('shard', None, 'tensor')
Inputs may be any that keep to these rules, and one draw needn't show every extreme that they name: `owner_list`: each owner index is named by at most 2 blocks, and some index by exactly 2. `left_root`: each slot's matrix is symmetric. `right_root`: each slot's matrix is symmetric.
All inputs are finite; a program needn't handle non-finite values.
Results may differ from a plain program's by a relative error of at most 0.0022.
Values may be sent and summed in bfloat16 or wider, within the bound.
No kernel may reach another device: no remote copies, remote signals or barrier semaphores. Data moves between devices by JAX's collectives and lax.ppermute only.
A program may use at most 128 MiB of HBM per device.

v0:
```python
import jax
import jax.numpy as jnp
from jax import lax
from jax.experimental import pallas as pl
from jax.experimental.pallas import tpu as pltpu
from jax.sharding import PartitionSpec as P


stat_decay = 0.95
moment_decay = 0.95
learn_rate = 0.02
graft_eps = 1e-06

f32 = jnp.float32
bf16 = jnp.bfloat16
VM = pl.BlockSpec(memory_space=pltpu.VMEM)
SM = pl.BlockSpec(memory_space=pltpu.SMEM)
HB = pl.BlockSpec(memory_space=pltpu.HBM)

NN = (((1,), (0,)), ((), ()))
NT = (((1,), (1,)), ((), ()))
TN = (((0,), (0,)), ((), ()))


def dot(a, b, dims):
    return lax.dot_general(a, b, dims, preferred_element_type=f32)


WHOLE = 63


def params(mib, **kw):
    return pltpu.CompilerParams(vmem_limit_bytes=mib * 1024 * 1024, **kw)


def cost(flops, nbytes):
    return pl.CostEstimate(flops=int(flops), bytes_accessed=int(nbytes), transcendentals=0)


def fill_slots(owner_ref, table_ref):
    @pl.loop(0, table_ref.shape[0])
    def _(i):
        table_ref[i] = -1

    @pl.loop(0, owner_ref.shape[0])
    def _(b):
        first = 2 * owner_ref[b]
        rank = (table_ref[first] >= 0).astype(jnp.int32)
        table_ref[first + rank] = b


def pick_kernel(rank, owner_ref, grad_ref, out_hbm, table_ref, wide_ref, out_ref, sem):
    fill_slots(owner_ref, table_ref)
    wide_ref[...] = pltpu.einshape("rbc->brc", grad_ref[...].astype(f32))

    @pl.loop(0, out_ref.shape[0])
    def _(d):
        b = table_ref[2 * d + rank]

        @pl.when(b >= 0)
        def _():
            out_ref[d] = wide_ref[b].astype(bf16)

        @pl.when(b < 0)
        def _():
            out_ref[d] = jnp.zeros(out_ref.shape[1:], bf16)

    pltpu.make_async_copy(out_ref, out_hbm, sem).start()
    pltpu.make_async_copy(out_ref, out_hbm, sem).wait()


def pick(rank, owner_list, gradients, shards):
    rows, nb, width = gradients.shape
    return pl.pallas_call(
        lambda *refs: pick_kernel(rank, *refs),
        out_shape=jax.ShapeDtypeStruct((shards, rows, width), bf16),
        in_specs=[SM, VM],
        out_specs=HB,
        scratch_shapes=[
            pltpu.SMEM((2 * shards,), jnp.int32),
            pltpu.VMEM((nb, rows, width), f32),
            pltpu.VMEM((shards, rows, width), bf16),
            pltpu.SemaphoreType.DMA,
        ],
        compiler_params=params(WHOLE),
        cost_estimate=cost(0, 5 * gradients.size),
    )(owner_list, gradients)


def turn_kernel(got_ref, out_hbm, wide_ref, out_ref, sem):
    count, rows, _ = got_ref.shape
    for s in range(count):
        wide_ref[s * rows : (s + 1) * rows, :] = got_ref[s].astype(f32)
    out_ref[...] = wide_ref[...].T.astype(bf16)
    pltpu.make_async_copy(out_ref, out_hbm, sem).start()
    pltpu.make_async_copy(out_ref, out_hbm, sem).wait()


def turn(got):
    count, rows, width = got.shape
    return pl.pallas_call(
        turn_kernel,
        out_shape=jax.ShapeDtypeStruct((width, count * rows), bf16),
        in_specs=[VM],
        out_specs=HB,
        scratch_shapes=[
            pltpu.VMEM((count * rows, width), f32),
            pltpu.VMEM((width, count * rows), bf16),
            pltpu.SemaphoreType.DMA,
        ],
        compiler_params=params(WHOLE),
        cost_estimate=cost(0, 5 * got.size),
        name="turn",
    )(got)


def moment_kernel(slot, grad_ref, mom_ref, *refs):
    out_ref, sum_ref = refs[slot:]
    g = grad_ref[...].astype(f32)
    v = moment_decay * mom_ref[0] + ((1.0 - moment_decay) * g) * g
    out_ref[0] = v
    d = g * lax.rsqrt(v)
    sum_ref[...] = jnp.broadcast_to(jnp.sum(d * d, keepdims=True), sum_ref.shape)


def moments(slot, grad, mom, before=()):
    _, part, wide = mom.shape
    block = pl.BlockSpec((1, part, wide), lambda n: (slot, 0, 0))
    return pl.pallas_call(
        lambda *refs: moment_kernel(slot, *refs),
        grid=(1,),
        out_shape=(
            jax.ShapeDtypeStruct(mom.shape, f32),
            jax.ShapeDtypeStruct((8, 128), f32),
        ),
        in_specs=[pl.BlockSpec((part, wide), lambda n: (0, 0)), block] + [HB] * len(before),
        out_specs=(block, pl.BlockSpec((8, 128), lambda n: (0, 0))),
        input_output_aliases={2 + i: i for i in range(len(before))},
        compiler_params=params(WHOLE),
        cost_estimate=cost(5 * mom.size, 5 * mom.size),
    )(grad, mom, *before)


def lane_block(n):
    return (n + 127) // 128 * 128


def cut_kernel(pos_ref, rows_ref, plus_ref, minus_ref, pad_ref):
    slots, part, wide = rows_ref.shape
    count = wide // part
    gap = pad_ref.shape[1] // count
    pos = pos_ref[0]
    for s in range(slots):
        for k in range(count):
            pad_ref[:, k * gap : k * gap + part] = rows_ref[s, :, k * part : (k + 1) * part]

        def block(step):
            start = pl.multiple_of(lax.rem(pos + step, count) * gap, 128)
            return pad_ref[:, pl.ds(start, gap)][:, :part]

        diag = block(0)
        for j, value in enumerate((block(3), diag, block(2))):
            at = (3 * s + j) * part
            plus_ref[:, at : at + part] = value
        mine = slice(s * part, (s + 1) * part)
        minus_ref[:part, mine] = diag
        minus_ref[part:, mine] = block(1)


def cut(pos, rows):
    slots, part, wide = rows.shape
    return pl.pallas_call(
        cut_kernel,
        out_shape=(
            jax.ShapeDtypeStruct((part, 3 * slots * part), bf16),
            jax.ShapeDtypeStruct((2 * part, slots * part), bf16),
        ),
        in_specs=[SM, VM],
        out_specs=(VM, VM),
        scratch_shapes=[pltpu.VMEM((part, wide // part * lane_block(part)), bf16)],
        compiler_params=params(WHOLE),
        cost_estimate=cost(0, 8 * rows.size),
        name="cut",
    )(pos, rows)


def patch_kernel(shards, s, pos_ref, rows_ref, plus_ref, minus_ref, far_ref, out_hbm, out_ref, sem):
    part, wide = rows_ref.shape[1:]
    count = wide // part
    gap = out_ref.shape[1] // count
    each = wide // shards
    pos = pos_ref[0]
    row = lax.broadcasted_iota(jnp.int32, (part, gap), 0)
    col = lax.broadcasted_iota(jnp.int32, (part, gap), 1)
    place = (col == (row // each) * lifted(each) + lax.rem(row, each)).astype(f32).astype(bf16)

    def put(a, b, value, flip):
        rows = pl.ds(pl.multiple_of(a * part, 16), part)
        at = pl.ds(pl.multiple_of(b * gap, 128), gap)
        out_ref[rows, at] = dot(value, place, TN if flip else NN).astype(bf16)

    def at(step):
        return lax.rem(pos + step, count)

    for k in range(count):
        own = rows_ref[0, :, k * part : (k + 1) * part]
        put(pos, k, own, False)
        put(k, pos, own, True)
    edge = plus_ref[:, 3 * s * part : (3 * s + 1) * part]
    put(at(3), at(2), edge, False)
    put(at(2), at(3), edge, True)
    put(at(3), at(3), plus_ref[:, (3 * s + 1) * part : (3 * s + 2) * part], False)
    edge = plus_ref[:, (3 * s + 2) * part : (3 * s + 3) * part]
    put(at(3), at(1), edge, False)
    put(at(1), at(3), edge, True)
    mine = slice(s * part, (s + 1) * part)
    put(at(1), at(1), minus_ref[:part, mine], False)
    put(at(1), at(2), minus_ref[part:, mine], False)
    put(at(2), at(1), minus_ref[part:, mine], True)
    put(at(2), at(2), far_ref[:, mine], False)
    copy = pltpu.make_async_copy(out_ref, out_hbm, sem)
    copy.start()
    copy.wait()


def lifted(n):
    return (n + 7) // 8 * 8


def patch(slot, pos, shards, rows, plus, minus, far):
    _, part, wide = rows.shape
    count = wide // part
    gap = lane_block(shards // count * lifted(wide // shards))
    shape = (wide, count * gap)

    def whole(x):
        return pl.BlockSpec(x.shape, lambda n: (0, 0))

    return pl.pallas_call(
        lambda *refs: patch_kernel(shards, slot, *refs),
        grid=(1,),
        out_shape=jax.ShapeDtypeStruct(shape, bf16),
        in_specs=[
            SM,
            pl.BlockSpec((1, part, wide), lambda n: (slot, 0, 0)),
            whole(plus),
            whole(minus),
            whole(far),
        ],
        out_specs=HB,
        scratch_shapes=[pltpu.VMEM(shape, bf16), pltpu.SemaphoreType.DMA],
        compiler_params=params(WHOLE),
        cost_estimate=cost(wide * wide * part, 3 * wide * wide),
    )(pos, rows, plus, minus, far)


def spread(pos, count, parts, full_ref, sems):
    part = parts[0].shape[0]
    copies = []
    for i, (piece, step) in enumerate(zip(parts, (0, count - 1, 1, 2))):
        start = pl.multiple_of(lax.rem(pos + step, count) * part, 16)
        copies.append(
            pltpu.make_async_copy(piece, full_ref.at[pl.ds(start, part), :], sems.at[i])
        )
    return copies


def pieces_of(value):
    high = value.astype(bf16).astype(f32)
    rest = jnp.where(high < 3e38, value - high, 0.0)
    mid = rest.astype(bf16).astype(f32)
    return high, mid, rest - mid


def precond_kernel(count, slot, *refs):
    pos_ref, right_ref, adam_ref, root_ref = refs[:4]
    grads = refs[4:8]
    out_hbm = refs[8]
    full_ref, root_buf, right_buf, prod_ref, pre_ref, out_ref, sems = refs[9:]
    first = spread(pos_ref[0], count, grads, full_ref, sems)
    first.append(pltpu.make_async_copy(right_ref.at[slot], right_buf, sems.at[4]))
    second = pltpu.make_async_copy(root_ref, root_buf, sems.at[5])
    for c in first:
        c.start()
    second.start()
    part, wide = right_buf.shape
    gap = root_buf.shape[1] // count
    for c in first:
        c.wait()
    step = wide // 3
    for n in range(3):
        cols = slice(n * step, (n + 1) * step)
        prod_ref[:, cols] = dot(right_buf[...], full_ref[:, cols], NN).astype(bf16)
    second.wait()
    total = jnp.zeros((1, 1), f32)
    for k in range(count):
        got = dot(prod_ref[...], root_buf[:, k * gap : (k + 1) * gap], NN)
        pre_ref[k] = got
        total = total + jnp.sum(got * got, keepdims=True)
    used, lanes = out_ref.shape[1:]
    rows = lax.broadcasted_iota(jnp.int32, (lanes - part, used), 0)
    extra = jnp.zeros((lanes - part, used), f32)
    for i, value in enumerate(pieces_of(total) + pieces_of(adam_ref[0:1, 0:1])):
        extra = jnp.where(rows == i, value, extra)
    for k in range(count):
        both = jnp.concatenate([pre_ref[k][:, :used], extra], axis=0)
        out_ref[k] = both.T.astype(bf16)
    last = pltpu.make_async_copy(out_ref, out_hbm, sems.at[0])
    last.start()
    last.wait()


def precondition(pos, count, shards, slot, right, adam, root, grads):
    part, wide = grads[0].shape
    long = root.shape[1]
    gap = long // count
    used = shards // count * lifted(wide // shards)
    lanes = lane_block(part)
    return pl.pallas_call(
        lambda *refs: precond_kernel(count, slot, *refs),
        out_shape=jax.ShapeDtypeStruct((count, used, lanes), bf16),
        in_specs=[SM, HB, VM, HB] + [HB] * 4,
        out_specs=HB,
        scratch_shapes=[
            pltpu.VMEM((wide, wide), bf16),
            pltpu.VMEM((wide, long), bf16),
            pltpu.VMEM((part, wide), bf16),
            pltpu.VMEM((part, wide), bf16),
            pltpu.VMEM((count, part, gap), f32),
            pltpu.VMEM((count, used, lanes), bf16),
            pltpu.SemaphoreType.DMA((6,)),
        ],
        compiler_params=params(WHOLE),
        cost_estimate=cost(4 * part * wide * wide, 4 * wide * wide),
    )(pos, right, adam, root, *grads)


def gram_kernel(count, slot, *refs):
    pos_ref, left_ref, right_ref = refs[:3]
    grads = refs[3:7]
    outl_ref, outr_ref, full_ref, own_ref, sems = refs[7 + 2 * slot :]
    n = pl.program_id(0)
    pos = pos_ref[0]
    wide = full_ref.shape[1]
    part = own_ref.shape[1]
    step = outl_ref.shape[2]

    @pl.when(n == 0)
    def _():
        copies = spread(pos, count, grads, full_ref, sems)
        for c in copies:
            c.start()
        for c in copies:
            c.wait()
        for k in range(count):

            @pl.when(pos == k)
            def _():
                own_ref[...] = full_ref[:, k * part : (k + 1) * part]

    cols = pl.ds(pl.multiple_of(n * step, 128), step)
    left = dot(own_ref[...], full_ref[:, cols], TN)
    outl_ref[0] = stat_decay * left_ref[0] + left / wide
    mine = full_ref[pl.ds(pl.multiple_of(pos * part, 16), part), :]
    right = dot(mine, full_ref[cols, :], NT)
    outr_ref[0] = stat_decay * right_ref[0] + right / wide


def grams(pos, count, slot, left, right, grads, before=()):
    _, part, wide = left.shape
    step = wide // 3
    block = pl.BlockSpec((1, part, step), lambda n: (slot, 0, n))
    shape = jax.ShapeDtypeStruct(left.shape, f32)
    return pl.pallas_call(
        lambda *refs: gram_kernel(count, slot, *refs),
        grid=(3,),
        out_shape=(shape, shape),
        in_specs=[SM, block, block] + [HB] * (4 + len(before)),
        out_specs=(block, block),
        scratch_shapes=[
            pltpu.VMEM((wide, wide), bf16),
            pltpu.VMEM((wide, part), bf16),
            pltpu.SemaphoreType.DMA((4,)),
        ],
        input_output_aliases={7 + i: i for i in range(len(before))},
        compiler_params=params(WHOLE),
        cost_estimate=cost(4 * part * wide * wide, 20 * part * wide),
    )(pos, left, right, *grads, *before)


def sums_kernel(at, back0_ref, back1_ref, out_ref):
    shards, _, lanes = back0_ref.shape
    lane = lax.broadcasted_iota(jnp.int32, (shards, lanes), 1)
    kept = jnp.zeros((shards, lanes), f32)
    for slot, back in enumerate((back0_ref, back1_ref)):
        first = back[...].astype(f32)[:, 0, :]
        for i in range(2):
            terms = [first[:, at + 3 * i + j : at + 3 * i + j + 1] for j in range(3)]
            kept = jnp.where(lane == 2 * slot + i, terms[0] + terms[1] + terms[2], kept)
    out_ref[...] = jnp.concatenate([kept.T[:8], jnp.zeros((8, lanes - shards), f32)], axis=1)


def partial_sums(part, back0, back1):
    shards = back0.shape[0]
    block = pl.BlockSpec((shards, 8, 128), lambda n: (0, 0, part // 128))
    return pl.pallas_call(
        lambda *refs: sums_kernel(part % 128, *refs),
        grid=(1,),
        out_shape=jax.ShapeDtypeStruct((8, 128), f32),
        in_specs=[block, block],
        out_specs=pl.BlockSpec((8, 128), lambda n: (0, 0)),
        compiler_params=params(8),
        name="sums",
    )(back0, back1)


def place_kernel(owner_ref, back0_ref, back1_ref, out_ref, where_ref, table_ref, wide_ref):
    fill_slots(owner_ref, table_ref)
    rows, _, part = out_ref.shape
    lane = lax.broadcasted_iota(jnp.int32, (1, where_ref.shape[2]), 1)
    where_ref[...] = jnp.zeros(where_ref.shape, f32)

    @pl.loop(0, back0_ref.shape[0])
    def _(d):
        for rank, back_ref in enumerate((back0_ref, back1_ref)):
            b = table_ref[2 * d + rank]

            @pl.when(b >= 0)
            def _():
                wide_ref[b] = back_ref[d, :, :part].astype(f32)
                where_ref[rank, pl.ds(b, 1), :] = (lane == d).astype(f32)

    out_ref[...] = pltpu.einshape("brc->rbc", wide_ref[...])[:rows]


def place(owner_list, backs, rows, part):
    nb = owner_list.shape[0]
    shards, lift = backs[0].shape[:2]
    return pl.pallas_call(
        place_kernel,
        out_shape=(
            jax.ShapeDtypeStruct((rows, nb, part), f32),
            jax.ShapeDtypeStruct((2, nb, 128), f32),
        ),
        in_specs=[SM, VM, VM],
        out_specs=(VM, VM),
        scratch_shapes=[
            pltpu.SMEM((2 * shards,), jnp.int32),
            pltpu.VMEM((nb, lift, part), f32),
        ],
        compiler_params=params(8),
        cost_estimate=cost(0, 8 * rows * nb * part),
        name="place",
    )(owner_list, *backs)


def final_kernel(entries, s0_ref, s1_ref, where_ref, dir_ref, w_ref, out_ref):
    total = (s0_ref[...] + s1_ref[...]) / entries

    def factor(rank):
        pre_mean, adam_mean = total[2 * rank : 2 * rank + 1], total[2 * rank + 1 : 2 * rank + 2]
        return -learn_rate * (jnp.sqrt(adam_mean) / jnp.sqrt(pre_mean + graft_eps))

    chosen = where_ref[0] * factor(0) + where_ref[1] * factor(1)
    scale = jnp.sum(chosen, axis=1, keepdims=True)
    for r in range(out_ref.shape[0]):
        out_ref[r] = w_ref[r] + scale * dir_ref[r]


def final(sums, where, direction, weights, entries):
    return pl.pallas_call(
        lambda *refs: final_kernel(entries, *refs),
        out_shape=jax.ShapeDtypeStruct(weights.shape, f32),
        in_specs=[VM] * 5,
        out_specs=VM,
        compiler_params=params(8),
        name="final",
    )(*sums, where, direction, weights)


def step(gradients, weights, owner_list, left_stats, right_stats, left_root, right_root, moment):
    shards = lax.axis_size("shard")
    count = lax.axis_size("tensor")
    pos = lax.axis_index("tensor").astype(jnp.int32).reshape(1)

    def shift(x, by):
        ring = [(i, (i + by) % count) for i in range(count)]
        return lax.ppermute(x, "tensor", ring)

    def exchange(x):
        return lax.all_to_all(x, "shard", 0, 0, tiled=True)

    left_rows = jnp.swapaxes(left_root, 1, 2)
    right_rows = jnp.swapaxes(right_root, 1, 2)
    grad_rows = jnp.swapaxes(gradients, 0, 1)
    mom_rows = jnp.swapaxes(moment, 1, 2)
    part, wide = left_rows.shape[1:]

    plus, minus = cut(pos, left_rows)
    plus, minus = shift(plus, 1), shift(minus, -1)
    far = shift(minus[:part], -1)

    parts, grads = [], []
    for s in range(2):
        send = pick(s, owner_list, grad_rows, shards)
        own = turn(exchange(send))
        l, r = shift(own, 1), shift(own, -1)
        far_part = shift(l, 1) if s == 0 else shift(r, -1)
        parts.append(own)
        grads.append((own, l, r, far_part))
    before, roots, adams, backs = (), [], [], []
    for s in range(2):
        new_moment, adam = moments(s, parts[s], mom_rows, before)
        before = (new_moment,)
        adams.append(adam)
        roots.append(patch(s, pos, shards, left_rows, plus, minus, far))
    for s in range(2):
        update = precondition(pos, count, shards, s, right_rows, adams[s], roots[s], grads[s])
        backs.append(exchange(update.reshape(shards, -1, update.shape[2])))
    stats = ()
    for s in range(2):
        stats = grams(pos, count, s, left_stats, right_stats, grads[s], stats)
    new_left, new_right = stats
    mine = partial_sums(part, backs[0], backs[1])

    def swap(x, flip):
        pairs = [(i, i ^ flip) for i in range(count)]
        return lax.ppermute(x, "tensor", pairs)

    mine = mine + swap(mine, 1)
    sums = [mine, swap(mine, 3)]
    rows = weights.shape[1]
    direction, where = place(owner_list, backs, rows, part)
    w_rows = jnp.swapaxes(weights, 0, 1)
    new_weights = final(sums, where, direction, w_rows, float(wide * wide))
    return (
        jnp.swapaxes(new_weights, 0, 1),
        new_left,
        new_right,
        jnp.swapaxes(new_moment, 1, 2),
    )


def solution(mesh):
    return jax.shard_map(
        step,
        mesh=mesh,
        in_specs=(
            P(None, "shard", "tensor"),
            P(None, "shard", "tensor"),
            P(),
            P("shard", "tensor", None),
            P("shard", "tensor", None),
            P("shard", None, "tensor"),
            P("shard", None, "tensor"),
            P("shard", None, "tensor"),
        ),
        out_specs=(
            P(None, "shard", "tensor"),
            P("shard", "tensor", None),
            P("shard", "tensor", None),
            P("shard", None, "tensor"),
        ),
        check_vma=False,
    )
```

profile of v0, /device:TPU:1, one launch (start us, length us, event | category | flops | bytes accessed | tf_op | source)
XLA Modules:
  0.0 182.6 jit_solution(17656254638860746276)
XLA Ops:
  0.6 4.1 %shard_map.115 = bf16[32,36,288]{2,1,0:T(8,128)(2,1)} custom-call(s32[32]{0:T(128)} %owner_ref.1, bf16[36,32,288]{2,1,0:T(8,128)(2,1)} %bitcast.20), custom_call_target="tpu_custom_call" | custom-call | bytes 1658880 | tf_op jit(solution)/shard_map/pallas_call | solution.py:74
  4.7 25.8 %all_to_all.20.got_ref = bf16[32,36,288]{2,1,0:T(8,128)(2,1)} all-to-all(bf16[32,36,288]{2,1,0:T(8,128)(2,1)} %shard_map.115), channel_id=1, replica_groups=mesh['shard'=32,'tensor'=4] {'shard'}, dimensions={0} | all-to-all | bytes 1327104 | tf_op jit(solution)/shard_map/all_to_all | solution.py:491
  30.5 2.4 %turn.3.refs_0_.refs_4_.refs_3_ = bf16[288,1152]{1,0:T(8,128)(2,1)} custom-call(bf16[32,36,288]{2,1,0:T(8,128)(2,1)} %all_to_all.20.got_ref), custom_call_target="tpu_custom_call" | custom-call | bytes 1658880 | tf_op jit(solution)/shard_map/turn/pallas_call | solution.py:101
  32.9 2.8 %collective-permute-start.7 = (bf16[288,1152]{1,0:T(8,128)(2,1)}, bf16[288,1152]{1,0:T(8,128)(2,1)}, u32[]{:S(2)}, u32[]{:S(2)}) collective-permute-start(bf16[288,1152]{1,0:T(8,128)(2,1)} %turn.3.refs_0_.refs_4_.refs_3_), channel_id=1, source_target_pairs={{0,3},{1,0},{2,1},{3,2},{4,7},{5,4},{6,5},{7,6},{8,11},{9,8},{10,9... | collective-permute-start | bytes 1990664 | tf_op jit(solution)/shard_map/ppermute | solution.py:488
  35.7 3.6 %cut.1 = (bf16[288,1728]{1,0:T(8,128)(2,1)}, bf16[576,576]{1,0:T(8,128)(2,1)}) custom-call(s32[1]{0:T(128)} %bitcast.pos_ref.refs_0_, bf16[2,288,1152]{2,1,0:T(8,128)(2,1)} %bitcast.11), custom_call_target="tpu_custom_call" | custom-call | bytes 5308416 | tf_op jit(solution)/shard_map/cut/pallas_call | solution.py:172
  39.3 0.4 collective-permute-start.1
  39.7 1.0 collective-permute-start
  40.7 4.1 %shard_map.111 = bf16[32,36,288]{2,1,0:T(8,128)(2,1)} custom-call(s32[32]{0:T(128)} %owner_ref.1, bf16[36,32,288]{2,1,0:T(8,128)(2,1)} %bitcast.21), custom_call_target="tpu_custom_call" | custom-call | bytes 1658880 | tf_op jit(solution)/shard_map/pallas_call | solution.py:74
  44.8 5.1 %all-to-all-start = ((bf16[32,36,288]{2,1,0:T(8,128)(2,1)}), bf16[32,36,288]{2,1,0:T(8,128)(2,1)}, u32[]{:S(2)}, u32[]{:S(2)}) async-start(bf16[32,36,288]{2,1,0:T(8,128)(2,1)} %shard_map.111), calls=%async_computation | async-start | bytes 1966080 | tf_op jit(solution)/shard_map/all_to_all | solution.py:491
  50.0 0.1 collective-permute-start.6
  50.1 0.1 collective-permute-done.7.refs_6_.refs_5_
  50.2 3.4 %collective-permute-start.8 = (bf16[288,1152]{1,0:T(8,128)(2,1)}, bf16[288,1152]{1,0:T(8,128)(2,1)}, u32[]{:S(2)}, u32[]{:S(2)}) collective-permute-start(bf16[288,1152]{1,0:T(8,128)(2,1)} %collective-permute-done.7.refs_6_.refs_5_), channel_id=1, source_target_pairs={{0,3},{1,0},{2,1},{3,2},{4,7},{5,4},{6,5},{7,6},{8,11},{9,8},{10,9... | collective-permute-start | bytes 1990664 | tf_op jit(solution)/shard_map/ppermute | solution.py:488
  53.6 12.8 %all-to-all-done.got_ref = bf16[32,36,288]{2,1,0:T(8,128)(2,1)} async-done(((bf16[32,36,288]{2,1,0:T(8,128)(2,1)}), bf16[32,36,288]{2,1,0:T(8,128)(2,1)}, u32[]{:S(2)}, u32[]{:S(2)}) %all-to-all-start) | async-done | bytes 663584 | tf_op jit(solution)/shard_map/all_to_all | solution.py:491
  66.4 2.4 %turn.2.refs_0_.refs_4_.refs_3_ = bf16[288,1152]{1,0:T(8,128)(2,1)} custom-call(bf16[32,36,288]{2,1,0:T(8,128)(2,1)} %all-to-all-done.got_ref), custom_call_target="tpu_custom_call" | custom-call | bytes 1658880 | tf_op jit(solution)/shard_map/turn/pallas_call | solution.py:101
  68.8 0.1 collective-permute-start.3
  68.9 0.0 collective-permute-done.1.refs_3_
  68.9 1.8 slice.4
  70.7 2.7 %collective-permute-start.2 = (bf16[288,576]{1,0:T(8,128)(2,1)}, bf16[288,576]{1,0:T(8,128)(2,1)}, u32[]{:S(2)}, u32[]{:S(2)}) collective-permute-start(bf16[288,576]{1,0:T(8,128)(2,1)} %slice.4), channel_id=1, source_target_pairs={{0,3},{1,0},{2,1},{3,2},{4,7},{5,4},{6,5},{7,6},{8,11},{9,8},{10,9... | collective-permute-start | bytes 995336 | tf_op jit(solution)/shard_map/ppermute | solution.py:488
  73.3 3.0 %shard_map.112 = (f32[2,288,1152]{2,1,0:T(8,128)}, f32[8,128]{1,0:T(8,128)}) custom-call(bf16[288,1152]{1,0:T(8,128)(2,1)} %turn.2.refs_0_.refs_4_.refs_3_, f32[2,288,1152]{2,1,0:T(8,128)} %bitcast.14), custom_call_target="tpu_custom_call" | custom-call | flops 3317760 | bytes 3317760 | tf_op jit(solution)/shard_map/pallas_call | solution.py:129
  76.4 3.0 %shard_map.116 = (f32[2,288,1152]{2,1,0:T(8,128)}, f32[8,128]{1,0:T(8,128)}) custom-call(bf16[288,1152]{1,0:T(8,128)(2,1)} %turn.3.refs_0_.refs_4_.refs_3_, f32[2,288,1152]{2,1,0:T(8,128)} %bitcast.15, f32[2,288,1152]{2,1,0:T(8,128)} %get-tuple-element.19.refs_2_), custom_call_target="tpu_custom_call", output_to_operand_aliasing={{0}: (2, {})} | custom-call | flops 3317760 | bytes 3317760 | tf_op jit(solution)/shard_map/pallas_call | solution.py:129
  79.4 8.7 %collective-permute-done.2.refs_4_ = bf16[288,576]{1,0:T(8,128)(2,1)} collective-permute-done((bf16[288,576]{1,0:T(8,128)(2,1)}, bf16[288,576]{1,0:T(8,128)(2,1)}, u32[]{:S(2)}, u32[]{:S(2)}) %collective-permute-start.2) | collective-permute-done | bytes 331808 | tf_op jit(solution)/shard_map/ppermute | solution.py:488
  88.1 0.0 collective-permute-done.refs_2_
  88.1 6.0 %shard_map.117.refs_3_ = bf16[1152,1536]{1,0:T(8,128)(2,1)} custom-call(s32[1]{0:T(128)} %bitcast.pos_ref.refs_0_, bf16[2,288,1152]{2,1,0:T(8,128)(2,1)} %bitcast.12, bf16[288,1728]{1,0:T(8,128)(2,1)} %collective-permute-done.refs_2_, bf16[576,576]{1,0:T(8,128)(2,1)} %collective-permute-done.1.refs_3_, bf16[288,576]{1,0:T(8,128)(2,1)} %collective-permute-done.2.refs_4_), custom_call_target="tpu_custom_call" | custom-call | flops 382205952 | bytes 3981312 | tf_op jit(solution)/shard_map/pallas_call | solution.py:239
  94.1 0.0 collective-permute-done.6.refs_5_.refs_4_
  94.1 0.0 collective-permute-done.8.refs_7_.refs_6_
  94.1 6.9 %shard_map.118 = bf16[4,320,384]{2,1,0:T(8,128)(2,1)} custom-call(s32[1]{0:T(128)} %bitcast.pos_ref.refs_0_, bf16[2,288,1152]{2,1,0:T(8,128)(2,1)} %bitcast.16, f32[8,128]{1,0:T(8,128)} %get-tuple-element.20.refs_2_, bf16[1152,1536]{1,0:T(8,128)(2,1)} %shard_map.117.refs_3_, bf16[288,1152]{1,0:T(8,128)(2,1)} %turn.3.refs_0_.refs_4_.refs_3_, ...), custom_call_target="tpu_custom_call" | custom-call | flops 1528823808 | bytes 5308416 | tf_op jit(solution)/shard_map/pallas_call | solution.py:319
  101.1 4.5 %all-to-all-start.3 = ((bf16[32,40,384]{2,1,0:T(8,128)(2,1)}), bf16[32,40,384]{2,1,0:T(8,128)(2,1)S(1)}, u32[]{:S(2)}, u32[]{:S(2)}) async-start(bf16[32,40,384]{2,1,0:T(8,128)(2,1)} %bitcast.18), calls=%async_computation.3 | async-start | bytes 1966080 | tf_op jit(solution)/shard_map/all_to_all | solution.py:491
  105.6 3.5 %collective-permute-start.4 = (bf16[288,1152]{1,0:T(8,128)(2,1)}, bf16[288,1152]{1,0:T(8,128)(2,1)}, u32[]{:S(2)}, u32[]{:S(2)}) collective-permute-start(bf16[288,1152]{1,0:T(8,128)(2,1)} %turn.2.refs_0_.refs_4_.refs_3_), channel_id=1, source_target_pairs={{0,3},{1,0},{2,1},{3,2},{4,7},{5,4},{6,5},{7,6},{8,11},{9,8},{10,9... | collective-permute-start | bytes 1990664 | tf_op jit(solution)/shard_map/ppermute | solution.py:488
  109.0 0.0 collective-permute-done.3.refs_5_.refs_4_
  109.1 0.0 collective-permute-start.5
  109.1 6.0 %shard_map.113.refs_3_ = bf16[1152,1536]{1,0:T(8,128)(2,1)} custom-call(s32[1]{0:T(128)} %bitcast.pos_ref.refs_0_, bf16[2,288,1152]{2,1,0:T(8,128)(2,1)} %bitcast.13, bf16[288,1728]{1,0:T(8,128)(2,1)} %collective-permute-done.refs_2_, bf16[576,576]{1,0:T(8,128)(2,1)} %collective-permute-done.1.refs_3_, bf16[288,576]{1,0:T(8,128)(2,1)} %collective-permute-done.2.refs_4_), custom_call_target="tpu_custom_call" | custom-call | flops 382205952 | bytes 3981312 | tf_op jit(solution)/shard_map/pallas_call | solution.py:239
  115.0 8.3 %collective-permute-done.4.refs_6_.refs_5_ = bf16[288,1152]{1,0:T(8,128)(2,1)} collective-permute-done((bf16[288,1152]{1,0:T(8,128)(2,1)}, bf16[288,1152]{1,0:T(8,128)(2,1)}, u32[]{:S(2)}, u32[]{:S(2)}) %collective-permute-start.4) | collective-permute-done | bytes 663584 | tf_op jit(solution)/shard_map/ppermute | solution.py:488
  123.3 3.1 %collective-permute-done.5.refs_7_.refs_6_ = bf16[288,1152]{1,0:T(8,128)(2,1)} collective-permute-done((bf16[288,1152]{1,0:T(8,128)(2,1)}, bf16[288,1152]{1,0:T(8,128)(2,1)}, u32[]{:S(2)}, u32[]{:S(2)}) %collective-permute-start.5) | collective-permute-done | bytes 663584 | tf_op jit(solution)/shard_map/ppermute | solution.py:488
  126.4 6.9 %shard_map.114 = bf16[4,320,384]{2,1,0:T(8,128)(2,1)} custom-call(s32[1]{0:T(128)} %bitcast.pos_ref.refs_0_, bf16[2,288,1152]{2,1,0:T(8,128)(2,1)} %bitcast.17, f32[8,128]{1,0:T(8,128)} %get-tuple-element.16.refs_2_, bf16[1152,1536]{1,0:T(8,128)(2,1)} %shard_map.113.refs_3_, bf16[288,1152]{1,0:T(8,128)(2,1)} %turn.2.refs_0_.refs_4_.refs_3_, ...), custom_call_target="tpu_custom_call" | custom-call | flops 1528823808 | bytes 5308416 | tf_op jit(solution)/shard_map/pallas_call | solution.py:319
  133.4 24.8 %all_to_all.21.refs_0_.back0_ref = bf16[32,40,384]{2,1,0:T(8,128)(2,1)S(1)} all-to-all(bf16[32,40,384]{2,1,0:T(8,128)(2,1)} %bitcast.19), channel_id=1, replica_groups=mesh['shard'=32,'tensor'=4] {'shard'}, dimensions={0} | all-to-all | bytes 1966080 | tf_op jit(solution)/shard_map/all_to_all | solution.py:491
  158.2 1.1 sums.1
  159.3 0.9 copy-done
  160.2 0.0 collective-permute-start.9
  160.2 7.1 %shard_map.119 = (f32[2,288,1152]{2,1,0:T(8,128)}, f32[2,288,1152]{2,1,0:T(8,128)}) custom-call(s32[1]{0:T(128)} %bitcast.pos_ref.refs_0_, f32[2,288,1152]{2,1,0:T(8,128)} %refs_1_.3, f32[2,288,1152]{2,1,0:T(8,128)} %refs_2_.3, bf16[288,1152]{1,0:T(8,128)(2,1)} %turn.2.refs_0_.refs_4_.refs_3_, bf16[288,1152]{1,0:T(8,128)(2,1)} %collective-permute-done.3.refs_5_.refs_4_, ...), custom_call_target="tpu_custom_call" | custom-call | flops 1528823808 | bytes 6635520 | tf_op jit(solution)/shard_map/pallas_call | solution.py:374
  167.3 0.0 collective-permute-done.9
  167.3 1.3 add.3.refs_0_
  168.6 0.3 collective-permute-start.10
  168.9 7.1 %shard_map.120 = (f32[2,288,1152]{2,1,0:T(8,128)}, f32[2,288,1152]{2,1,0:T(8,128)}) custom-call(s32[1]{0:T(128)} %bitcast.pos_ref.refs_0_, f32[2,288,1152]{2,1,0:T(8,128)} %refs_1_.3, f32[2,288,1152]{2,1,0:T(8,128)} %refs_2_.3, bf16[288,1152]{1,0:T(8,128)(2,1)} %turn.3.refs_0_.refs_4_.refs_3_, ...), custom_call_target="tpu_custom_call", output_to_operand_aliasing={{0}: (7, {}), {1}: (8, {})} | custom-call | flops 1528823808 | bytes 6635520 | tf_op jit(solution)/shard_map/pallas_call | solution.py:374
  176.0 0.0 copy-start.1
  176.0 1.2 copy-done.1
  177.2 0.7 copy-done.3
  177.9 2.6 %place.1 = (f32[36,32,288]{2,1,0:T(8,128)S(1)}, f32[2,32,128]{2,1,0:T(8,128)S(1)}) custom-call(s32[32]{0:T(128)S(1)} %copy-done.3, bf16[32,40,384]{2,1,0:T(8,128)(2,1)S(1)} %copy-done.1, bf16[32,40,384]{2,1,0:T(8,128)(2,1)S(1)} %all-to-all-done.3.refs_1_.back1_ref), custom_call_target="tpu_custom_call" | custom-call | bytes 2654208 | tf_op jit(solution)/shard_map/place/pallas_call | solution.py:439
  180.5 2.2 %final.1 = f32[36,32,288]{2,1,0:T(8,128)} custom-call(f32[8,128]{1,0:T(8,128)} %add.3.refs_0_, f32[8,128]{1,0:T(8,128)} %collective-permute-done.10.refs_1_, f32[2,32,128]{2,1,0:T(8,128)S(1)} %get-tuple-element.21.refs_2_, f32[36,32,288]{2,1,0:T(8,128)S(1)} %get-tuple-element.22.refs_3_, f32[36,32,288]{2,1,0:T(8,128)S(1)} %bitcast.10), custom_call_target="tpu_custom_call" | custom-call | tf_op jit(solution)/shard_map/final/pallas_call | solution.py:471
  (8 shorter events, 0.0 us)
Async XLA Ops:
  32.9 17.1 %copy-start.4 = (bf16[288,1152]{1,0:T(8,128)(2,1)S(1)}, bf16[288,1152]{1,0:T(8,128)(2,1)}, u32[]{:S(2)}) copy-start(bf16[288,1152]{1,0:T(8,128)(2,1)} %turn.3.refs_0_.refs_4_.refs_3_) | copy-start | bytes 1990660
  32.9 17.3 %collective-permute-start.7 = (bf16[288,1152]{1,0:T(8,128)(2,1)}, bf16[288,1152]{1,0:T(8,128)(2,1)}, u32[]{:S(2)}, u32[]{:S(2)}) collective-permute-start(bf16[288,1152]{1,0:T(8,128)(2,1)} %turn.3.refs_0_.refs_4_.refs_3_), channel_id=1, source_target_pairs={{0,3},{1,0},{2,1},{3,2},{4,7},{5,4},{6,5},{7,6},{8,11},{9,8},{10,9... | collective-permute-start | bytes 1990664 | tf_op jit(solution)/shard_map/ppermute | solution.py:488
  39.3 29.6 %collective-permute-start.1 = (bf16[576,576]{1,0:T(8,128)(2,1)}, bf16[576,576]{1,0:T(8,128)(2,1)}, u32[]{:S(2)}, u32[]{:S(2)}) collective-permute-start(bf16[576,576]{1,0:T(8,128)(2,1)} %get-tuple-element.18), channel_id=1, source_target_pairs={{0,3},{1,0},{2,1},{3,2},{4,7},{5,4},{6,5},{7,6},{8,11},{9,8},{10,9... | collective-permute-start | bytes 1990664 | tf_op jit(solution)/shard_map/ppermute | solution.py:488
  39.7 48.4 %collective-permute-start = (bf16[288,1728]{1,0:T(8,128)(2,1)}, bf16[288,1728]{1,0:T(8,128)(2,1)}, u32[]{:S(2)}, u32[]{:S(2)}) collective-permute-start(bf16[288,1728]{1,0:T(8,128)(2,1)} %get-tuple-element.17), channel_id=1, source_target_pairs={{0,1},{1,2},{2,3},{3,0},{4,5},{5,6},{6,7},{7,4},{8,9},{9,10},{10,1... | collective-permute-start | bytes 2985992 | tf_op jit(solution)/shard_map/ppermute | solution.py:488
  44.8 21.5 %all-to-all-start = ((bf16[32,36,288]{2,1,0:T(8,128)(2,1)}), bf16[32,36,288]{2,1,0:T(8,128)(2,1)}, u32[]{:S(2)}, u32[]{:S(2)}) async-start(bf16[32,36,288]{2,1,0:T(8,128)(2,1)} %shard_map.111), calls=%async_computation | async-start | bytes 1966080 | tf_op jit(solution)/shard_map/all_to_all | solution.py:491
  50.0 44.1 %collective-permute-start.6 = (bf16[288,1152]{1,0:T(8,128)(2,1)S(1)}, bf16[288,1152]{1,0:T(8,128)(2,1)}, u32[]{:S(2)}, u32[]{:S(2)}) collective-permute-start(bf16[288,1152]{1,0:T(8,128)(2,1)S(1)} %copy-done.4), channel_id=1, source_target_pairs={{0,1},{1,2},{2,3},{3,0},{4,5},{5,6},{6,7},{7,4},{8,9},{9,10},{10,1... | collective-permute-start | bytes 1990664 | tf_op jit(solution)/shard_map/ppermute | solution.py:488
  50.2 43.9 %collective-permute-start.8 = (bf16[288,1152]{1,0:T(8,128)(2,1)}, bf16[288,1152]{1,0:T(8,128)(2,1)}, u32[]{:S(2)}, u32[]{:S(2)}) collective-permute-start(bf16[288,1152]{1,0:T(8,128)(2,1)} %collective-permute-done.7.refs_6_.refs_5_), channel_id=1, source_target_pairs={{0,3},{1,0},{2,1},{3,2},{4,7},{5,4},{6,5},{7,6},{8,11},{9,8},{10,9... | collective-permute-start | bytes 1990664 | tf_op jit(solution)/shard_map/ppermute | solution.py:488
  68.8 40.2 %collective-permute-start.3 = (bf16[288,1152]{1,0:T(8,128)(2,1)}, bf16[288,1152]{1,0:T(8,128)(2,1)}, u32[]{:S(2)}, u32[]{:S(2)}) collective-permute-start(bf16[288,1152]{1,0:T(8,128)(2,1)} %turn.2.refs_0_.refs_4_.refs_3_), channel_id=1, source_target_pairs={{0,1},{1,2},{2,3},{3,0},{4,5},{5,6},{6,7},{7,4},{8,9},{9,10},{10,1... | collective-permute-start | bytes 1990664 | tf_op jit(solution)/shard_map/ppermute | solution.py:488
  70.7 17.5 %collective-permute-start.2 = (bf16[288,576]{1,0:T(8,128)(2,1)}, bf16[288,576]{1,0:T(8,128)(2,1)}, u32[]{:S(2)}, u32[]{:S(2)}) collective-permute-start(bf16[288,576]{1,0:T(8,128)(2,1)} %slice.4), channel_id=1, source_target_pairs={{0,3},{1,0},{2,1},{3,2},{4,7},{5,4},{6,5},{7,6},{8,11},{9,8},{10,9... | collective-permute-start | bytes 995336 | tf_op jit(solution)/shard_map/ppermute | solution.py:488
  101.1 32.3 %all-to-all-start.3 = ((bf16[32,40,384]{2,1,0:T(8,128)(2,1)}), bf16[32,40,384]{2,1,0:T(8,128)(2,1)S(1)}, u32[]{:S(2)}, u32[]{:S(2)}) async-start(bf16[32,40,384]{2,1,0:T(8,128)(2,1)} %bitcast.18), calls=%async_computation.3 | async-start | bytes 1966080 | tf_op jit(solution)/shard_map/all_to_all | solution.py:491
  105.6 17.7 %collective-permute-start.4 = (bf16[288,1152]{1,0:T(8,128)(2,1)}, bf16[288,1152]{1,0:T(8,128)(2,1)}, u32[]{:S(2)}, u32[]{:S(2)}) collective-permute-start(bf16[288,1152]{1,0:T(8,128)(2,1)} %turn.2.refs_0_.refs_4_.refs_3_), channel_id=1, source_target_pairs={{0,3},{1,0},{2,1},{3,2},{4,7},{5,4},{6,5},{7,6},{8,11},{9,8},{10,9... | collective-permute-start | bytes 1990664 | tf_op jit(solution)/shard_map/ppermute | solution.py:488
  109.1 17.4 %collective-permute-start.5 = (bf16[288,1152]{1,0:T(8,128)(2,1)}, bf16[288,1152]{1,0:T(8,128)(2,1)}, u32[]{:S(2)}, u32[]{:S(2)}) collective-permute-start(bf16[288,1152]{1,0:T(8,128)(2,1)} %collective-permute-done.3.refs_5_.refs_4_), channel_id=1, source_target_pairs={{0,1},{1,2},{2,3},{3,0},{4,5},{5,6},{6,7},{7,4},{8,9},{9,10},{10,1... | collective-permute-start | bytes 1990664 | tf_op jit(solution)/shard_map/ppermute | solution.py:488
  159.3 0.9 copy-start
  160.2 7.1 %collective-permute-start.9 = (f32[8,128]{1,0:T(8,128)}, f32[8,128]{1,0:T(8,128)}, u32[]{:S(2)}, u32[]{:S(2)}) collective-permute-start(f32[8,128]{1,0:T(8,128)} %sums.1), channel_id=1, source_target_pairs={{0,1},{1,0},{2,3},{3,2},{4,5},{5,4},{6,7},{7,6},{8,9},{9,8},{10,11... | collective-permute-start | bytes 12296 | tf_op jit(solution)/shard_map/ppermute | solution.py:528
  168.6 11.8 %collective-permute-start.10 = (f32[8,128]{1,0:T(8,128)}, f32[8,128]{1,0:T(8,128)}, u32[]{:S(2)}, u32[]{:S(2)}) collective-permute-start(f32[8,128]{1,0:T(8,128)} %add.3.refs_0_), channel_id=1, source_target_pairs={{0,3},{1,2},{2,1},{3,0},{4,7},{5,6},{6,5},{7,4},{8,11},{9,10},{10,... | collective-permute-start | bytes 12296 | tf_op jit(solution)/shard_map/ppermute | solution.py:528
  176.0 1.2 copy-start.1
  177.2 0.7 copy-start.3
  177.9 2.6 %copy-start.2 = (f32[32,36,288]{2,0,1:T(8,128)S(1)}, f32[32,36,288]{2,0,1:T(8,128)}, u32[]{:S(2)}) copy-start(f32[32,36,288]{2,0,1:T(8,128)} %param.9) | copy-start | bytes 3981316
where the time goes:
time: 184 us; the launch traced here: 183 us
  Pallas kernels  68.4 us (37%)
  blocking collectives  50.6 us (28%)
  waiting for transfers between devices  33 us (18%)
  starting transfers between devices  23.9 us (13%)
  local copies, waits for them, and re-layouts  4.56 us (2%)
    all_to_all x2, blocking collectives, exchange(): return lax.all_to_all(x, 'shard', 0, 0, tiled=True)  50.6 us
    ppermute x9, waiting for transfers between devices, shift(): return lax.ppermute(x, 'tensor', ring)  20.2 us
    pallas_call x2, Pallas kernels, grams(): pl.pallas_call(lambda *refs: gram_kernel(count, slot, *refs), grid=(3,),...  14.2 us
    ppermute x9, starting transfers between devices, shift(): return lax.ppermute(x, 'tensor', ring)  14 us
    pallas_call x2, Pallas kernels, precondition(): pl.pallas_call(lambda *refs: precond_kernel(count, slot, *refs), out_shap...  13.9 us
    all_to_all x2, waiting for transfers between devices, exchange(): return lax.all_to_all(x, 'shard', 0, 0, tiled=True)  12.8 us
    pallas_call x2, Pallas kernels, patch(): pl.pallas_call(lambda *refs: patch_kernel(shards, slot, *refs), grid=(1,)...  11.9 us
    all_to_all x2, starting transfers between devices, exchange(): return lax.all_to_all(x, 'shard', 0, 0, tiled=True)  9.66 us
  transfers between devices with their start and end apart: 13, of which 5 were waited for; matrix products, arithmetic and copies ran while one was open for 1% of the time, Pallas kernels for 32%

commit v1 on v0

--- a/solution.py
+++ b/solution.py
@@ -49,9 +49,37 @@
         table_ref[first + rank] = b
 
 
+PACKED = 88
+
+
+def pack(x, extra=None):
+    row = lax.broadcasted_iota(jnp.int32, (8, 128), 0)
+    lane = lax.broadcasted_iota(jnp.int32, (8, 128), 1)
+    tail = x[:, 256:384]
+    wrapped = tail[0:8]
+    for j in range(1, 4):
+        turned = pltpu.roll(tail[8 * j : 8 * j + 8], 32 * j, 1)
+        wrapped = jnp.where(lane >= 32 * j, turned, wrapped)
+    low = jnp.where(row < 4, x[32:40, 0:128], pltpu.roll(x[32:40, 128:256], 4, 0))
+    last = tail[32:40] if extra is None else jnp.where(lane < 32, tail[32:40], extra)
+    return jnp.concatenate([x[0:32, 0:128], x[0:32, 128:256], wrapped, low, last], axis=0)
+
+
+def unpack(y, put):
+    put(0, 0, y[0:32])
+    put(0, 128, y[32:64])
+    for j in range(4):
+        part = y[64:72] if j == 0 else pltpu.roll(y[64:72], 128 - 32 * j, 1)
+        put(8 * j, 256, part[:, :32])
+    put(32, 0, y[72:76])
+    put(32, 128, pltpu.roll(y[72:80], 4, 0)[0:4])
+    put(32, 256, y[80:84, :32])
+
+
 def pick_kernel(rank, owner_ref, grad_ref, out_hbm, table_ref, wide_ref, out_ref, sem):
     fill_slots(owner_ref, table_ref)
-    wide_ref[...] = pltpu.einshape("rbc->brc", grad_ref[...].astype(f32))
+    rows, _, width = grad_ref.shape
+    wide_ref[:, :rows, :width] = pltpu.einshape("rbc->brc", grad_ref[...].astype(f32))
 
     @pl.loop(0, out_ref.shape[0])
     def _(d):
@@ -59,7 +87,7 @@
 
         @pl.when(b >= 0)
         def _():
-            out_ref[d] = wide_ref[b].astype(bf16)
+            out_ref[d] = pack(wide_ref[b]).astype(bf16)
 
         @pl.when(b < 0)
         def _():
@@ -70,16 +98,16 @@
 
 
 def pick(rank, owner_list, gradients, shards):
-    rows, nb, width = gradients.shape
+    _, nb, _ = gradients.shape
     return pl.pallas_call(
         lambda *refs: pick_kernel(rank, *refs),
-        out_shape=jax.ShapeDtypeStruct((shards, rows, width), bf16),
+        out_shape=jax.ShapeDtypeStruct((shards, PACKED, 128), bf16),
         in_specs=[SM, VM],
         out_specs=HB,
         scratch_shapes=[
             pltpu.SMEM((2 * shards,), jnp.int32),
-            pltpu.VMEM((nb, rows, width), f32),
-            pltpu.VMEM((shards, rows, width), bf16),
+            pltpu.VMEM((nb, 40, 384), f32),
+            pltpu.VMEM((shards, PACKED, 128), bf16),
             pltpu.SemaphoreType.DMA,
         ],
         compiler_params=params(WHOLE),
@@ -88,16 +116,22 @@
 
 
 def turn_kernel(got_ref, out_hbm, wide_ref, out_ref, sem):
-    count, rows, _ = got_ref.shape
+    count = got_ref.shape[0]
+    rows = wide_ref.shape[0] // count
     for s in range(count):
-        wide_ref[s * rows : (s + 1) * rows, :] = got_ref[s].astype(f32)
+
+        def put(row, column, value):
+            at = s * rows + row
+            wide_ref[at : at + value.shape[0], column : column + value.shape[1]] = value
+
+        unpack(got_ref[s].astype(f32), put)
     out_ref[...] = wide_ref[...].T.astype(bf16)
     pltpu.make_async_copy(out_ref, out_hbm, sem).start()
     pltpu.make_async_copy(out_ref, out_hbm, sem).wait()
 
 
-def turn(got):
-    count, rows, width = got.shape
+def turn(got, rows, width):
+    count = got.shape[0]
     return pl.pallas_call(
         turn_kernel,
         out_shape=jax.ShapeDtypeStruct((width, count * rows), bf16),
@@ -108,7 +142,7 @@
             pltpu.VMEM((width, count * rows), bf16),
             pltpu.SemaphoreType.DMA,
         ],
-        compiler_params=params(WHOLE),
+        compiler_params=params(8),
         cost_estimate=cost(0, 5 * got.size),
         name="turn",
     )(got)
@@ -136,7 +170,7 @@
         in_specs=[pl.BlockSpec((part, wide), lambda n: (0, 0)), block] + [HB] * len(before),
         out_specs=(block, pl.BlockSpec((8, 128), lambda n: (0, 0))),
         input_output_aliases={2 + i: i for i in range(len(before))},
-        compiler_params=params(WHOLE),
+        compiler_params=params(24),
         cost_estimate=cost(5 * mom.size, 5 * mom.size),
     )(grad, mom, *before)
 
@@ -249,7 +283,7 @@
         ],
         out_specs=HB,
         scratch_shapes=[pltpu.VMEM(shape, bf16), pltpu.SemaphoreType.DMA],
-        compiler_params=params(WHOLE),
+        compiler_params=params(24),
         cost_estimate=cost(wide * wide * part, 3 * wide * wide),
     )(pos, rows, plus, minus, far)
 
@@ -272,7 +306,7 @@
     return high, mid, rest - mid
 
 
-def precond_kernel(count, slot, *refs):
+def precond_kernel(count, shards, slot, *refs):
     pos_ref, right_ref, adam_ref, root_ref = refs[:4]
     grads = refs[4:8]
     out_hbm = refs[8]
@@ -297,14 +331,17 @@
         got = dot(prod_ref[...], root_buf[:, k * gap : (k + 1) * gap], NN)
         pre_ref[k] = got
         total = total + jnp.sum(got * got, keepdims=True)
-    used, lanes = out_ref.shape[1:]
-    rows = lax.broadcasted_iota(jnp.int32, (lanes - part, used), 0)
-    extra = jnp.zeros((lanes - part, used), f32)
+    lane = lax.broadcasted_iota(jnp.int32, (8, 128), 1)
+    extra = jnp.zeros((8, 128), f32)
     for i, value in enumerate(pieces_of(total) + pieces_of(adam_ref[0:1, 0:1])):
-        extra = jnp.where(rows == i, value, extra)
+        extra = jnp.where(lane == 32 + i, value, extra)
+    lift = lifted(wide // shards)
+    blank = jnp.zeros((lane_block(part) - part, gap), f32)
     for k in range(count):
-        both = jnp.concatenate([pre_ref[k][:, :used], extra], axis=0)
-        out_ref[k] = both.T.astype(bf16)
+        turned = jnp.concatenate([pre_ref[k], blank], axis=0).T
+        for j in range(shards // count):
+            block = pack(turned[j * lift : (j + 1) * lift], extra)
+            out_ref[k * (shards // count) + j] = block.astype(bf16)
     last = pltpu.make_async_copy(out_ref, out_hbm, sems.at[0])
     last.start()
     last.wait()
@@ -314,11 +351,9 @@
     part, wide = grads[0].shape
     long = root.shape[1]
     gap = long // count
-    used = shards // count * lifted(wide // shards)
-    lanes = lane_block(part)
-    return pl.pallas_call(
-        lambda *refs: precond_kernel(count, slot, *refs),
-        out_shape=jax.ShapeDtypeStruct((count, used, lanes), bf16),
+    return pl.pallas_call(
+        lambda *refs: precond_kernel(count, shards, slot, *refs),
+        out_shape=jax.ShapeDtypeStruct((shards, PACKED, 128), bf16),
         in_specs=[SM, HB, VM, HB] + [HB] * 4,
         out_specs=HB,
         scratch_shapes=[
@@ -327,7 +362,7 @@
             pltpu.VMEM((part, wide), bf16),
             pltpu.VMEM((part, wide), bf16),
             pltpu.VMEM((count, part, gap), f32),
-            pltpu.VMEM((count, used, lanes), bf16),
+            pltpu.VMEM((shards, PACKED, 128), bf16),
             pltpu.SemaphoreType.DMA((6,)),
         ],
         compiler_params=params(WHOLE),
@@ -388,23 +423,23 @@
     )(pos, left, right, *grads, *before)
 
 
-def sums_kernel(at, back0_ref, back1_ref, out_ref):
+def sums_kernel(back0_ref, back1_ref, out_ref):
     shards, _, lanes = back0_ref.shape
     lane = lax.broadcasted_iota(jnp.int32, (shards, lanes), 1)
     kept = jnp.zeros((shards, lanes), f32)
     for slot, back in enumerate((back0_ref, back1_ref)):
         first = back[...].astype(f32)[:, 0, :]
         for i in range(2):
-            terms = [first[:, at + 3 * i + j : at + 3 * i + j + 1] for j in range(3)]
+            terms = [first[:, 32 + 3 * i + j : 33 + 3 * i + j] for j in range(3)]
             kept = jnp.where(lane == 2 * slot + i, terms[0] + terms[1] + terms[2], kept)
     out_ref[...] = jnp.concatenate([kept.T[:8], jnp.zeros((8, lanes - shards), f32)], axis=1)
 
 
-def partial_sums(part, back0, back1):
+def partial_sums(back0, back1):
     shards = back0.shape[0]
-    block = pl.BlockSpec((shards, 8, 128), lambda n: (0, 0, part // 128))
-    return pl.pallas_call(
-        lambda *refs: sums_kernel(part % 128, *refs),
+    block = pl.BlockSpec((shards, 8, 128), lambda n: (0, PACKED // 8 - 1, 0))
+    return pl.pallas_call(
+        sums_kernel,
         grid=(1,),
         out_shape=jax.ShapeDtypeStruct((8, 128), f32),
         in_specs=[block, block],
@@ -416,7 +451,7 @@
 
 def place_kernel(owner_ref, back0_ref, back1_ref, out_ref, where_ref, table_ref, wide_ref):
     fill_slots(owner_ref, table_ref)
-    rows, _, part = out_ref.shape
+    rows, _, _ = out_ref.shape
     lane = lax.broadcasted_iota(jnp.int32, (1, where_ref.shape[2]), 1)
     where_ref[...] = jnp.zeros(where_ref.shape, f32)
 
@@ -427,7 +462,12 @@
 
             @pl.when(b >= 0)
             def _():
-                wide_ref[b] = back_ref[d, :, :part].astype(f32)
+
+                def put(row, column, value):
+                    height, width = value.shape
+                    wide_ref[b, row : row + height, column : column + width] = value
+
+                unpack(back_ref[d].astype(f32), put)
                 where_ref[rank, pl.ds(b, 1), :] = (lane == d).astype(f32)
 
     out_ref[...] = pltpu.einshape("brc->rbc", wide_ref[...])[:rows]
@@ -435,7 +475,7 @@
 
 def place(owner_list, backs, rows, part):
     nb = owner_list.shape[0]
-    shards, lift = backs[0].shape[:2]
+    shards = backs[0].shape[0]
     return pl.pallas_call(
         place_kernel,
         out_shape=(
@@ -446,7 +486,7 @@
         out_specs=(VM, VM),
         scratch_shapes=[
             pltpu.SMEM((2 * shards,), jnp.int32),
-            pltpu.VMEM((nb, lift, part), f32),
+            pltpu.VMEM((nb, lifted(rows), part), f32),
         ],
         compiler_params=params(8),
         cost_estimate=cost(0, 8 * rows * nb * part),
@@ -503,7 +543,7 @@
     parts, grads = [], []
     for s in range(2):
         send = pick(s, owner_list, grad_rows, shards)
-        own = turn(exchange(send))
+        own = turn(exchange(send), gradients.shape[1], part)
         l, r = shift(own, 1), shift(own, -1)
         far_part = shift(l, 1) if s == 0 else shift(r, -1)
         parts.append(own)
@@ -516,12 +556,12 @@
         roots.append(patch(s, pos, shards, left_rows, plus, minus, far))
     for s in range(2):
         update = precondition(pos, count, shards, s, right_rows, adams[s], roots[s], grads[s])
-        backs.append(exchange(update.reshape(shards, -1, update.shape[2])))
+        backs.append(exchange(update))
     stats = ()
     for s in range(2):
         stats = grams(pos, count, s, left_stats, right_stats, grads[s], stats)
     new_left, new_right = stats
-    mine = partial_sums(part, backs[0], backs[1])
+    mine = partial_sums(backs[0], backs[1])
 
     def swap(x, flip):
         pairs = [(i, i ^ flip) for i in range(count)]

time: 184 us -> 180 us (0.978)
  blocking collectives: 50.6 us -> 21 us
  starting transfers between devices: 23.9 us -> 42.5 us
  local copies, waits for them, and re-layouts: 4.56 us -> 17 us
  Pallas kernels: 68.4 us -> 59.8 us
  waiting for transfers between devices: 33 us -> 37.8 us
    all_to_all x2 -> x1, blocking collectives: 50.6 us -> 21 us  [exchange(): return lax.all_to_all(x, 'shard', 0, 0, tiled=True)]
    unnamed x10 -> x44, local copies, waits for them, and re-layouts: 2.8 us -> 17 us
    all_to_all x2 -> x3, starting transfers between devices: 9.66 us -> 21.9 us  [exchange(): return lax.all_to_all(x, 'shard', 0, 0, tiled=True)]
    pallas_call x2, Pallas kernels: 11.9 us -> 5.85 us  [patch(): pl.pallas_call(lambda *refs: patch_kernel(shards, slot, *refs), grid=(1,)...]
    ppermute x9, waiting for transfers between devices: 20.2 us -> 25.4 us  [shift(): return lax.ppermute(x, 'tensor', ring)]
    ppermute x9, starting transfers between devices: 14 us -> 17.2 us  [shift(): return lax.ppermute(x, 'tensor', ring)]
    ppermute x2, starting transfers between devices: 0.31 us -> 3.35 us  [swap(): return lax.ppermute(x, 'tensor', pairs)]
    pallas_call x2, Pallas kernels: 6.1 us -> 4.12 us  [moments(): pl.pallas_call(lambda *refs: moment_kernel(slot, *refs), grid=(1,), out_s...]
  transfers between devices with their start and end apart: 13 -> 14, of which waited for: 5 -> 5; matrix products, arithmetic and copies ran while one was open for 1% -> 0% of each run, Pallas kernels for 32% -> 30%
where the time goes in v1:
time: 180 us; the launch traced here: 179 us
  Pallas kernels  59.8 us (33%)
  starting transfers between devices  42.5 us (24%)
  waiting for transfers between devices  37.8 us (21%)
  blocking collectives  21 us (12%)
  local copies, waits for them, and re-layouts  17 us (9%)
    ppermute x9, waiting for transfers between devices, shift(): return lax.ppermute(x, 'tensor', ring)  25.4 us
    all_to_all x3, starting transfers between devices, exchange(): return lax.all_to_all(x, 'shard', 0, 0, tiled=True)  21.9 us
    all_to_all x1, blocking collectives, exchange(): return lax.all_to_all(x, 'shard', 0, 0, tiled=True)  21 us
    ppermute x9, starting transfers between devices, shift(): return lax.ppermute(x, 'tensor', ring)  17.2 us
    unnamed x44, local copies, waits for them, and re-layouts  17 us
    pallas_call x2, Pallas kernels, grams(): pl.pallas_call(lambda *refs: gram_kernel(count, slot, *refs), grid=(3,),...  14.2 us
    pallas_call x2, Pallas kernels, precondition(): pl.pallas_call(lambda *refs: precond_kernel(count, shards, slot, *refs),...  13.7 us
    all_to_all x3, waiting for transfers between devices, exchange(): return lax.all_to_all(x, 'shard', 0, 0, tiled=True)  12.4 us
  transfers between devices with their start and end apart: 14, of which 5 were waited for; matrix products, arithmetic and copies ran while one was open for 0% of the time, Pallas kernels for 30%

profile of v1, /device:TPU:1, one launch (start us, length us, event | category | flops | bytes accessed | tf_op | source)
XLA Modules:
  0.0 178.9 jit_solution(7826193322730919709)
XLA Ops:
  0.6 4.4 %shard_map.115 = bf16[32,88,128]{2,1,0:T(8,128)(2,1)} custom-call(s32[32]{0:T(128)} %owner_ref.1, bf16[36,32,288]{2,1,0:T(8,128)(2,1)} %bitcast.16), custom_call_target="tpu_custom_call" | custom-call | bytes 1658880 | tf_op jit(solution)/shard_map/pallas_call | solution.py:102
  5.0 9.4 %all-to-all-start.2 = ((bf16[32,88,128]{2,1,0:T(8,128)(2,1)}), bf16[32,88,128]{2,1,0:T(8,128)(2,1)S(1)}, u32[]{:S(2)}, u32[]{:S(2)}) async-start(bf16[32,88,128]{2,1,0:T(8,128)(2,1)} %shard_map.115), calls=%async_computation.2 | async-start | bytes 1441792 | tf_op jit(solution)/shard_map/all_to_all | solution.py:531
  14.5 5.0 %shard_map.111 = bf16[32,88,128]{2,1,0:T(8,128)(2,1)} custom-call(s32[32]{0:T(128)} %owner_ref.1, bf16[36,32,288]{2,1,0:T(8,128)(2,1)} %bitcast.17), custom_call_target="tpu_custom_call" | custom-call | bytes 1658880 | tf_op jit(solution)/shard_map/pallas_call | solution.py:102
  19.5 8.5 %all-to-all-done.2.got_ref = bf16[32,88,128]{2,1,0:T(8,128)(2,1)S(1)} async-done(((bf16[32,88,128]{2,1,0:T(8,128)(2,1)}), bf16[32,88,128]{2,1,0:T(8,128)(2,1)S(1)}, u32[]{:S(2)}, u32[]{:S(2)}) %all-to-all-start.2) | async-done | bytes 720928 | tf_op jit(solution)/shard_map/all_to_all | solution.py:531
  28.0 0.9 copy-done.12
  28.9 4.4 %all-to-all-start = ((bf16[32,88,128]{2,1,0:T(8,128)(2,1)}), bf16[32,88,128]{2,1,0:T(8,128)(2,1)}, u32[]{:S(2)}, u32[]{:S(2)}) async-start(bf16[32,88,128]{2,1,0:T(8,128)(2,1)} %shard_map.111), calls=%async_computation | async-start | bytes 1441792 | tf_op jit(solution)/shard_map/all_to_all | solution.py:531
  33.3 1.1 copy-done.13
  34.4 0.6 turn.3.refs_0_.refs_4_.refs_3_
  35.0 2.8 %collective-permute-start.7 = (bf16[288,1152]{1,0:T(8,128)(2,1)S(1)}, bf16[288,1152]{1,0:T(8,128)(2,1)}, u32[]{:S(2)}, u32[]{:S(2)}) collective-permute-start(bf16[288,1152]{1,0:T(8,128)(2,1)S(1)} %turn.3.refs_0_.refs_4_.refs_3_), channel_id=1, source_target_pairs={{0,3},{1,0},{2,1},{3,2},{4,7},{5,4},{6,5},{7,6},{8,11},{9,8},{10,9... | collective-permute-start | bytes 1990664 | tf_op jit(solution)/shard_map/ppermute | solution.py:528
  37.8 3.6 %cut.1 = (bf16[288,1728]{1,0:T(8,128)(2,1)}, bf16[576,576]{1,0:T(8,128)(2,1)}) custom-call(s32[1]{0:T(128)} %bitcast.pos_ref.refs_0_, bf16[2,288,1152]{2,1,0:T(8,128)(2,1)} %bitcast.8), custom_call_target="tpu_custom_call" | custom-call | bytes 5308416 | tf_op jit(solution)/shard_map/cut/pallas_call | solution.py:206
  41.4 0.4 collective-permute-start.1
  41.9 1.0 collective-permute-start
  42.9 3.9 %all-to-all-done.got_ref = bf16[32,88,128]{2,1,0:T(8,128)(2,1)} async-done(((bf16[32,88,128]{2,1,0:T(8,128)(2,1)}), bf16[32,88,128]{2,1,0:T(8,128)(2,1)}, u32[]{:S(2)}, u32[]{:S(2)}) %all-to-all-start) | async-done | bytes 720928 | tf_op jit(solution)/shard_map/all_to_all | solution.py:531
  46.7 2.3 %turn.2.refs_0_.refs_4_.refs_3_ = bf16[288,1152]{1,0:T(8,128)(2,1)} custom-call(bf16[32,88,128]{2,1,0:T(8,128)(2,1)} %all-to-all-done.got_ref), custom_call_target="tpu_custom_call" | custom-call | bytes 1802240 | tf_op jit(solution)/shard_map/turn/pallas_call | solution.py:135
  49.1 1.4 collective-permute-start.3
  50.5 1.3 collective-permute-start.6
  51.8 0.2 collective-permute-done.7.refs_6_.refs_5_
  52.0 3.5 %collective-permute-start.8 = (bf16[288,1152]{1,0:T(8,128)(2,1)}, bf16[288,1152]{1,0:T(8,128)(2,1)S(1)}, u32[]{:S(2)}, u32[]{:S(2)}) collective-permute-start(bf16[288,1152]{1,0:T(8,128)(2,1)} %collective-permute-done.7.refs_6_.refs_5_), channel_id=1, source_target_pairs={{0,3},{1,0},{2,1},{3,2},{4,7},{5,4},{6,5},{7,6},{8,11},{9,8},{10,9... | collective-permute-start | bytes 1990664 | tf_op jit(solution)/shard_map/ppermute | solution.py:528
  55.5 12.4 %collective-permute-done.1.refs_3_ = bf16[576,576]{1,0:T(8,128)(2,1)S(1)} collective-permute-done((bf16[576,576]{1,0:T(8,128)(2,1)}, bf16[576,576]{1,0:T(8,128)(2,1)S(1)}, u32[]{:S(2)}, u32[]{:S(2)}) %collective-permute-start.1) | collective-permute-done | bytes 663584 | tf_op jit(solution)/shard_map/ppermute | solution.py:528
  67.9 3.4 %collective-permute-start.2 = (bf16[288,576]{1,0:T(8,128)(2,1)S(1)}, bf16[288,576]{1,0:T(8,128)(2,1)S(1)}, u32[]{:S(2)}, u32[]{:S(2)}) collective-permute-start(bf16[288,576]{1,0:T(8,128)(2,1)S(1)} %slice.4), channel_id=1, source_target_pairs={{0,3},{1,0},{2,1},{3,2},{4,7},{5,4},{6,5},{7,6},{8,11},{9,8},{10,9... | collective-permute-start | bytes 995336 | tf_op jit(solution)/shard_map/ppermute | solution.py:528
  71.3 1.7 copy-done.5
  73.1 2.6 %shard_map.112 = (f32[2,288,1152]{2,1,0:T(8,128)}, f32[8,128]{1,0:T(8,128)S(1)}) custom-call(bf16[288,1152]{1,0:T(8,128)(2,1)} %turn.2.refs_0_.refs_4_.refs_3_, f32[2,288,1152]{2,1,0:T(8,128)S(1)} %bitcast.11), custom_call_target="tpu_custom_call" | custom-call | flops 3317760 | bytes 3317760 | tf_op jit(solution)/shard_map/pallas_call | solution.py:163
  75.7 1.5 shard_map.116
  77.2 12.7 %collective-permute-done.2.refs_4_ = bf16[288,576]{1,0:T(8,128)(2,1)S(1)} collective-permute-done((bf16[288,576]{1,0:T(8,128)(2,1)S(1)}, bf16[288,576]{1,0:T(8,128)(2,1)S(1)}, u32[]{:S(2)}, u32[]{:S(2)}) %collective-permute-start.2) | collective-permute-done | bytes 331808 | tf_op jit(solution)/shard_map/ppermute | solution.py:528
  89.9 3.4 %collective-permute-start.4 = (bf16[288,1152]{1,0:T(8,128)(2,1)}, bf16[288,1152]{1,0:T(8,128)(2,1)}, u32[]{:S(2)}, u32[]{:S(2)}) collective-permute-start(bf16[288,1152]{1,0:T(8,128)(2,1)} %turn.2.refs_0_.refs_4_.refs_3_), channel_id=1, source_target_pairs={{0,3},{1,0},{2,1},{3,2},{4,7},{5,4},{6,5},{7,6},{8,11},{9,8},{10,9... | collective-permute-start | bytes 1990664 | tf_op jit(solution)/shard_map/ppermute | solution.py:528
  93.3 2.9 %shard_map.117.refs_3_ = bf16[1152,1536]{1,0:T(8,128)(2,1)S(1)} custom-call(s32[1]{0:T(128)} %bitcast.pos_ref.refs_0_, bf16[2,288,1152]{2,1,0:T(8,128)(2,1)S(1)} %bitcast.9, bf16[288,1728]{1,0:T(8,128)(2,1)S(1)} %collective-permute-done.refs_2_, bf16[576,576]{1,0:T(8,128)(2,1)S(1)} %collective-permute-done.1.refs_3_, ...), custom_call_target="tpu_custom_call" | custom-call | flops 382205952 | bytes 3981312 | tf_op jit(solution)/shard_map/pallas_call | solution.py:273
  96.3 1.7 copy-done
  98.1 0.8 copy-done.20
  98.9 0.9 copy-done.21
  99.8 6.9 %shard_map.118 = bf16[32,88,128]{2,1,0:T(8,128)(2,1)} custom-call(s32[1]{0:T(128)} %bitcast.pos_ref.refs_0_, bf16[2,288,1152]{2,1,0:T(8,128)(2,1)} %bitcast.14, f32[8,128]{1,0:T(8,128)} %copy-done.19, bf16[1152,1536]{1,0:T(8,128)(2,1)} %copy-done, bf16[288,1152]{1,0:T(8,128)(2,1)} %copy-done.4, bf16[288,1152]{1,0:T(8,128)(2,1)} %copy-done.20, ...), custom_call_target="tpu_custom_call" | custom-call | flops 1528823808 | bytes 5308416 | tf_op jit(solution)/shard_map/pallas_call | solution.py:354
  106.6 8.1 %all-to-all-start.3 = ((bf16[32,88,128]{2,1,0:T(8,128)(2,1)}), bf16[32,88,128]{2,1,0:T(8,128)(2,1)S(1)}, u32[]{:S(2)}, u32[]{:S(2)}) async-start(bf16[32,88,128]{2,1,0:T(8,128)(2,1)} %shard_map.118), calls=%async_computation.3 | async-start | bytes 1441792 | tf_op jit(solution)/shard_map/all_to_all | solution.py:531
  114.7 1.3 copy-done.3
  116.0 1.1 copy-done.9
  117.1 1.2 copy-done.11
  118.4 1.0 copy-done.16
  119.3 2.9 %shard_map.113.refs_3_ = bf16[1152,1536]{1,0:T(8,128)(2,1)S(1)} custom-call(s32[1]{0:T(128)} %bitcast.pos_ref.refs_0_, bf16[2,288,1152]{2,1,0:T(8,128)(2,1)S(1)} %bitcast.10, bf16[288,1728]{1,0:T(8,128)(2,1)S(1)} %copy-done.11, bf16[576,576]{1,0:T(8,128)(2,1)S(1)} %copy-done.9, bf16[288,576]{1,0:T(8,128)(2,1)S(1)} %copy-done.16), custom_call_target="tpu_custom_call" | custom-call | flops 382205952 | bytes 3981312 | tf_op jit(solution)/shard_map/pallas_call | solution.py:273
  122.3 1.7 copy-done.1
  124.0 6.8 %shard_map.114 = bf16[32,88,128]{2,1,0:T(8,128)(2,1)} custom-call(s32[1]{0:T(128)} %bitcast.pos_ref.refs_0_, bf16[2,288,1152]{2,1,0:T(8,128)(2,1)} %bitcast.15, f32[8,128]{1,0:T(8,128)} %copy-done.18, bf16[1152,1536]{1,0:T(8,128)(2,1)} %copy-done.1, bf16[288,1152]{1,0:T(8,128)(2,1)} %turn.2.refs_0_.refs_4_.refs_3_, ...), custom_call_target="tpu_custom_call" | custom-call | flops 1528823808 | bytes 5308416 | tf_op jit(solution)/shard_map/pallas_call | solution.py:354
  130.9 21.0 %all_to_all.20.back0_ref = bf16[32,88,128]{2,1,0:T(8,128)(2,1)S(1)} all-to-all(bf16[32,88,128]{2,1,0:T(8,128)(2,1)} %shard_map.114), channel_id=1, replica_groups=mesh['shard'=32,'tensor'=4] {'shard'}, dimensions={0} | all-to-all | bytes 1441792 | tf_op jit(solution)/shard_map/all_to_all | solution.py:531
  151.9 0.5 sums.1
  152.3 0.9 copy-done.6
  153.2 7.1 %shard_map.119 = (f32[2,288,1152]{2,1,0:T(8,128)}, f32[2,288,1152]{2,1,0:T(8,128)}) custom-call(s32[1]{0:T(128)} %bitcast.pos_ref.refs_0_, f32[2,288,1152]{2,1,0:T(8,128)} %refs_1_.3, f32[2,288,1152]{2,1,0:T(8,128)} %refs_2_.3, bf16[288,1152]{1,0:T(8,128)(2,1)} %turn.2.refs_0_.refs_4_.refs_3_, bf16[288,1152]{1,0:T(8,128)(2,1)} %collective-permute-done.3.refs_5_.refs_4_, ...), custom_call_target="tpu_custom_call" | custom-call | flops 1528823808 | bytes 6635520 | tf_op jit(solution)/shard_map/pallas_call | solution.py:409
  160.3 3.4 %collective-permute-start.10 = (f32[8,128]{1,0:T(8,128)S(1)}, f32[8,128]{1,0:T(8,128)S(1)}, u32[]{:S(2)}, u32[]{:S(2)}) collective-permute-start(f32[8,128]{1,0:T(8,128)S(1)} %add.3.refs_0_), channel_id=1, source_target_pairs={{0,3},{1,2},{2,1},{3,0},{4,7},{5,6},{6,5},{7,4},{8,11},{9,10},{10,... | collective-permute-start | bytes 12296 | tf_op jit(solution)/shard_map/ppermute | solution.py:568
  163.7 7.1 %shard_map.120 = (f32[2,288,1152]{2,1,0:T(8,128)}, f32[2,288,1152]{2,1,0:T(8,128)}) custom-call(s32[1]{0:T(128)} %bitcast.pos_ref.refs_0_, f32[2,288,1152]{2,1,0:T(8,128)} %refs_1_.3, f32[2,288,1152]{2,1,0:T(8,128)} %refs_2_.3, bf16[288,1152]{1,0:T(8,128)(2,1)} %copy-done.4, ...), custom_call_target="tpu_custom_call", output_to_operand_aliasing={{0}: (7, {}), {1}: (8, {})} | custom-call | flops 1528823808 | bytes 6635520 | tf_op jit(solution)/shard_map/pallas_call | solution.py:409
  170.8 1.1 copy-done.7
  171.9 4.1 %place.1 = (f32[36,32,288]{2,1,0:T(8,128)S(1)}, f32[2,32,128]{2,1,0:T(8,128)S(1)}) custom-call(s32[32]{0:T(128)S(1)} %copy-done.17, bf16[32,88,128]{2,1,0:T(8,128)(2,1)S(1)} %copy-done.7, bf16[32,88,128]{2,1,0:T(8,128)(2,1)S(1)} %all-to-all-done.3.back1_ref), custom_call_target="tpu_custom_call" | custom-call | bytes 2654208 | tf_op jit(solution)/shard_map/place/pallas_call | solution.py:479
  176.0 1.5 copy-done.14
  177.4 1.5 final.1
  (43 shorter events, 0.1 us)
Async XLA Ops:
  5.0 23.0 %all-to-all-start.2 = ((bf16[32,88,128]{2,1,0:T(8,128)(2,1)}), bf16[32,88,128]{2,1,0:T(8,128)(2,1)S(1)}, u32[]{:S(2)}, u32[]{:S(2)}) async-start(bf16[32,88,128]{2,1,0:T(8,128)(2,1)} %shard_map.115), calls=%async_computation.2 | async-start | bytes 1441792 | tf_op jit(solution)/shard_map/all_to_all | solution.py:531
  28.0 0.9 copy-start.12
  28.9 17.9 %all-to-all-start = ((bf16[32,88,128]{2,1,0:T(8,128)(2,1)}), bf16[32,88,128]{2,1,0:T(8,128)(2,1)}, u32[]{:S(2)}, u32[]{:S(2)}) async-start(bf16[32,88,128]{2,1,0:T(8,128)(2,1)} %shard_map.111), calls=%async_computation | async-start | bytes 1441792 | tf_op jit(solution)/shard_map/all_to_all | solution.py:531
  33.3 1.1 copy-start.13
  35.0 40.7 %copy-start.4 = (bf16[288,1152]{1,0:T(8,128)(2,1)}, bf16[288,1152]{1,0:T(8,128)(2,1)S(1)}, u32[]{:S(2)}) copy-start(bf16[288,1152]{1,0:T(8,128)(2,1)S(1)} %turn.3.refs_0_.refs_4_.refs_3_) | copy-start | bytes 1990660
  35.0 17.0 %collective-permute-start.7 = (bf16[288,1152]{1,0:T(8,128)(2,1)S(1)}, bf16[288,1152]{1,0:T(8,128)(2,1)}, u32[]{:S(2)}, u32[]{:S(2)}) collective-permute-start(bf16[288,1152]{1,0:T(8,128)(2,1)S(1)} %turn.3.refs_0_.refs_4_.refs_3_), channel_id=1, source_target_pairs={{0,3},{1,0},{2,1},{3,2},{4,7},{5,4},{6,5},{7,6},{8,11},{9,8},{10,9... | collective-permute-start | bytes 1990664 | tf_op jit(solution)/shard_map/ppermute | solution.py:528
  41.4 26.5 %collective-permute-start.1 = (bf16[576,576]{1,0:T(8,128)(2,1)}, bf16[576,576]{1,0:T(8,128)(2,1)S(1)}, u32[]{:S(2)}, u32[]{:S(2)}) collective-permute-start(bf16[576,576]{1,0:T(8,128)(2,1)} %get-tuple-element.18), channel_id=1, source_target_pairs={{0,3},{1,0},{2,1},{3,2},{4,7},{5,4},{6,5},{7,6},{8,11},{9,8},{10,9... | collective-permute-start | bytes 1990664 | tf_op jit(solution)/shard_map/ppermute | solution.py:528
  41.9 51.5 %collective-permute-start = (bf16[288,1728]{1,0:T(8,128)(2,1)}, bf16[288,1728]{1,0:T(8,128)(2,1)S(1)}, u32[]{:S(2)}, u32[]{:S(2)}) collective-permute-start(bf16[288,1728]{1,0:T(8,128)(2,1)} %get-tuple-element.17), channel_id=1, source_target_pairs={{0,1},{1,2},{2,3},{3,0},{4,5},{5,6},{6,7},{7,4},{8,9},{9,10},{10,1... | collective-permute-start | bytes 2985992 | tf_op jit(solution)/shard_map/ppermute | solution.py:528
  49.1 49.0 %collective-permute-start.3 = (bf16[288,1152]{1,0:T(8,128)(2,1)}, bf16[288,1152]{1,0:T(8,128)(2,1)}, u32[]{:S(2)}, u32[]{:S(2)}) collective-permute-start(bf16[288,1152]{1,0:T(8,128)(2,1)} %turn.2.refs_0_.refs_4_.refs_3_), channel_id=1, source_target_pairs={{0,1},{1,2},{2,3},{3,0},{4,5},{5,6},{6,7},{7,4},{8,9},{9,10},{10,1... | collective-permute-start | bytes 1990664 | tf_op jit(solution)/shard_map/ppermute | solution.py:528
  50.5 47.6 %collective-permute-start.6 = (bf16[288,1152]{1,0:T(8,128)(2,1)S(1)}, bf16[288,1152]{1,0:T(8,128)(2,1)S(1)}, u32[]{:S(2)}, u32[]{:S(2)}) collective-permute-start(bf16[288,1152]{1,0:T(8,128)(2,1)S(1)} %turn.3.refs_0_.refs_4_.refs_3_), channel_id=1, source_target_pairs={{0,1},{1,2},{2,3},{3,0},{4,5},{5,6},{6,7},{7,4},{8,9},{9,10},{10,1... | collective-permute-start | bytes 1990664 | tf_op jit(solution)/shard_map/ppermute | solution.py:528
  52.0 46.9 %collective-permute-start.8 = (bf16[288,1152]{1,0:T(8,128)(2,1)}, bf16[288,1152]{1,0:T(8,128)(2,1)S(1)}, u32[]{:S(2)}, u32[]{:S(2)}) collective-permute-start(bf16[288,1152]{1,0:T(8,128)(2,1)} %collective-permute-done.7.refs_6_.refs_5_), channel_id=1, source_target_pairs={{0,3},{1,0},{2,1},{3,2},{4,7},{5,4},{6,5},{7,6},{8,11},{9,8},{10,9... | collective-permute-start | bytes 1990664 | tf_op jit(solution)/shard_map/ppermute | solution.py:528
  67.9 25.4 %copy-start.8 = (bf16[576,576]{1,0:T(8,128)(2,1)}, bf16[576,576]{1,0:T(8,128)(2,1)S(1)}, u32[]{:S(2)}) copy-start(bf16[576,576]{1,0:T(8,128)(2,1)S(1)} %collective-permute-done.1.refs_3_) | copy-start | bytes 1990660
  67.9 22.0 %collective-permute-start.2 = (bf16[288,576]{1,0:T(8,128)(2,1)S(1)}, bf16[288,576]{1,0:T(8,128)(2,1)S(1)}, u32[]{:S(2)}, u32[]{:S(2)}) collective-permute-start(bf16[288,576]{1,0:T(8,128)(2,1)S(1)} %slice.4), channel_id=1, source_target_pairs={{0,3},{1,0},{2,1},{3,2},{4,7},{5,4},{6,5},{7,6},{8,11},{9,8},{10,9... | collective-permute-start | bytes 995336 | tf_op jit(solution)/shard_map/ppermute | solution.py:528
  71.3 1.7 copy-start.5
  75.7 1.5 copy-start.18
  75.7 17.7 %copy-start.2 = (bf16[2,1152,288]{1,2,0:T(8,128)(2,1)S(1)}, bf16[2,1152,288]{1,2,0:T(8,128)(2,1)}, u32[]{:S(2)}) copy-start(bf16[2,1152,288]{1,2,0:T(8,128)(2,1)} %param.13) | copy-start | bytes 3981316
  77.2 19.1 %copy-start.19 = (f32[8,128]{1,0:T(8,128)}, f32[8,128]{1,0:T(8,128)S(1)}, u32[]{:S(2)}) copy-start(f32[8,128]{1,0:T(8,128)S(1)} %get-tuple-element.20.refs_2_) | copy-start | bytes 12292
  89.9 6.4 %copy-start.15 = (bf16[288,576]{1,0:T(8,128)(2,1)}, bf16[288,576]{1,0:T(8,128)(2,1)S(1)}, u32[]{:S(2)}) copy-start(bf16[288,576]{1,0:T(8,128)(2,1)S(1)} %collective-permute-done.2.refs_4_) | copy-start | bytes 995332
  89.9 34.1 %collective-permute-start.4 = (bf16[288,1152]{1,0:T(8,128)(2,1)}, bf16[288,1152]{1,0:T(8,128)(2,1)}, u32[]{:S(2)}, u32[]{:S(2)}) collective-permute-start(bf16[288,1152]{1,0:T(8,128)(2,1)} %turn.2.refs_0_.refs_4_.refs_3_), channel_id=1, source_target_pairs={{0,3},{1,0},{2,1},{3,2},{4,7},{5,4},{6,5},{7,6},{8,11},{9,8},{10,9... | collective-permute-start | bytes 1990664 | tf_op jit(solution)/shard_map/ppermute | solution.py:528
  93.3 3.0 %copy-start.10 = (bf16[288,1728]{1,0:T(8,128)(2,1)}, bf16[288,1728]{1,0:T(8,128)(2,1)S(1)}, u32[]{:S(2)}) copy-start(bf16[288,1728]{1,0:T(8,128)(2,1)S(1)} %collective-permute-done.refs_2_) | copy-start | bytes 2985988
  96.3 1.7 copy-start
  98.1 26.0 %collective-permute-start.5 = (bf16[288,1152]{1,0:T(8,128)(2,1)}, bf16[288,1152]{1,0:T(8,128)(2,1)}, u32[]{:S(2)}, u32[]{:S(2)}) collective-permute-start(bf16[288,1152]{1,0:T(8,128)(2,1)} %collective-permute-done.3.refs_5_.refs_4_), channel_id=1, source_target_pairs={{0,1},{1,2},{2,3},{3,0},{4,5},{5,6},{6,7},{7,4},{8,9},{9,10},{10,1... | collective-permute-start | bytes 1990664 | tf_op jit(solution)/shard_map/ppermute | solution.py:528
  98.1 0.8 copy-start.20
  98.9 0.9 copy-start.21
  106.6 24.3 %all-to-all-start.3 = ((bf16[32,88,128]{2,1,0:T(8,128)(2,1)}), bf16[32,88,128]{2,1,0:T(8,128)(2,1)S(1)}, u32[]{:S(2)}, u32[]{:S(2)}) async-start(bf16[32,88,128]{2,1,0:T(8,128)(2,1)} %shard_map.118), calls=%async_computation.3 | async-start | bytes 1441792 | tf_op jit(solution)/shard_map/all_to_all | solution.py:531
  114.7 1.3 copy-start.3
  116.0 1.1 copy-start.9
  117.1 1.2 copy-start.11
  118.4 1.0 copy-start.16
  122.3 1.7 copy-start.1
  152.3 0.9 copy-start.6
  153.2 7.1 %collective-permute-start.9 = (f32[8,128]{1,0:T(8,128)S(1)}, f32[8,128]{1,0:T(8,128)S(1)}, u32[]{:S(2)}, u32[]{:S(2)}) collective-permute-start(f32[8,128]{1,0:T(8,128)S(1)} %sums.1), channel_id=1, source_target_pairs={{0,1},{1,0},{2,3},{3,2},{4,5},{5,4},{6,7},{7,6},{8,9},{9,8},{10,11... | collective-permute-start | bytes 12296 | tf_op jit(solution)/shard_map/ppermute | solution.py:568
  160.3 15.6 %collective-permute-start.10 = (f32[8,128]{1,0:T(8,128)S(1)}, f32[8,128]{1,0:T(8,128)S(1)}, u32[]{:S(2)}, u32[]{:S(2)}) collective-permute-start(f32[8,128]{1,0:T(8,128)S(1)} %add.3.refs_0_), channel_id=1, source_target_pairs={{0,3},{1,2},{2,1},{3,0},{4,7},{5,6},{6,5},{7,4},{8,11},{9,10},{10,... | collective-permute-start | bytes 12296 | tf_op jit(solution)/shard_map/ppermute | solution.py:568
  163.7 7.1 %copy-start.17 = (s32[32]{0:T(128)S(1)}, s32[32]{0:T(128)}, u32[]{:S(2)}) copy-start(s32[32]{0:T(128)} %owner_ref.1) | copy-start | bytes 388
  170.8 1.1 copy-start.7
  176.0 1.5 copy-start.14

commit v2 on v1

--- a/solution.py
+++ b/solution.py
@@ -76,39 +76,58 @@
     put(32, 256, y[80:84, :32])
 
 
-def pick_kernel(rank, owner_ref, grad_ref, out_hbm, table_ref, wide_ref, out_ref, sem):
+def pick_kernel(rank, owner_ref, grad_hbm, out_hbm, table_ref, grad_ref, wide_ref, out_ref, sems):
+    rows, _, width = grad_ref.shape
+    spans = (slice(0, 16), slice(16, rows))
+    loads = [
+        pltpu.make_async_copy(grad_hbm.at[x], grad_ref.at[x], sems.at[4 + i])
+        for i, x in enumerate(spans)
+    ]
+    for c in loads:
+        c.start()
     fill_slots(owner_ref, table_ref)
-    rows, _, width = grad_ref.shape
-    wide_ref[:, :rows, :width] = pltpu.einshape("rbc->brc", grad_ref[...].astype(f32))
-
-    @pl.loop(0, out_ref.shape[0])
-    def _(d):
-        b = table_ref[2 * d + rank]
-
-        @pl.when(b >= 0)
-        def _():
-            out_ref[d] = pack(wide_ref[b]).astype(bf16)
-
-        @pl.when(b < 0)
-        def _():
-            out_ref[d] = jnp.zeros(out_ref.shape[1:], bf16)
-
-    pltpu.make_async_copy(out_ref, out_hbm, sem).start()
-    pltpu.make_async_copy(out_ref, out_hbm, sem).wait()
+    for c, x in zip(loads, spans):
+        c.wait()
+        wide_ref[:, x, :width] = pltpu.einshape("rbc->brc", grad_ref[x].astype(f32))
+
+    per = out_ref.shape[0] // 4
+
+    def sent(i):
+        rows = pl.ds(i * per, per)
+        return pltpu.make_async_copy(out_ref.at[rows], out_hbm.at[rows], sems.at[i])
+
+    for i in range(4):
+
+        @pl.loop(i * per, (i + 1) * per)
+        def _(d):
+            b = table_ref[2 * d + rank]
+
+            @pl.when(b >= 0)
+            def _():
+                out_ref[d] = pack(wide_ref[b]).astype(bf16)
+
+            @pl.when(b < 0)
+            def _():
+                out_ref[d] = jnp.zeros(out_ref.shape[1:], bf16)
+
+        sent(i).start()
+    for i in range(4):
+        sent(i).wait()
 
 
 def pick(rank, owner_list, gradients, shards):
-    _, nb, _ = gradients.shape
+    rows, nb, width = gradients.shape
     return pl.pallas_call(
         lambda *refs: pick_kernel(rank, *refs),
         out_shape=jax.ShapeDtypeStruct((shards, PACKED, 128), bf16),
-        in_specs=[SM, VM],
+        in_specs=[SM, HB],
         out_specs=HB,
         scratch_shapes=[
             pltpu.SMEM((2 * shards,), jnp.int32),
+            pltpu.VMEM((rows, nb, width), bf16),
             pltpu.VMEM((nb, 40, 384), f32),
             pltpu.VMEM((shards, PACKED, 128), bf16),
-            pltpu.SemaphoreType.DMA,
+            pltpu.SemaphoreType.DMA((6,)),
         ],
         compiler_params=params(WHOLE),
         cost_estimate=cost(0, 5 * gradients.size),
@@ -179,11 +198,16 @@
     return (n + 127) // 128 * 128
 
 
-def cut_kernel(pos_ref, rows_ref, plus_ref, minus_ref, pad_ref):
-    slots, part, wide = rows_ref.shape
+def position():
+    return lax.axis_index("tensor").astype(jnp.int32)
+
+
+def cut_kernel(rows_ref, plus_ref, minus_ref, pad_ref):
+    slots, _, wide = rows_ref.shape
+    part = minus_ref.shape[2] // slots
     count = wide // part
     gap = pad_ref.shape[1] // count
-    pos = pos_ref[0]
+    pos = position()
     for s in range(slots):
         for k in range(count):
             pad_ref[:, k * gap : k * gap + part] = rows_ref[s, :, k * part : (k + 1) * part]
@@ -197,33 +221,39 @@
             at = (3 * s + j) * part
             plus_ref[:, at : at + part] = value
         mine = slice(s * part, (s + 1) * part)
-        minus_ref[:part, mine] = diag
-        minus_ref[part:, mine] = block(1)
-
-
-def cut(pos, rows):
+        minus_ref[0, :, mine] = diag
+        minus_ref[1, :, mine] = block(1)
+
+
+def cut(rows):
     slots, part, wide = rows.shape
-    return pl.pallas_call(
+    chunk = part
+    plus, minus = pl.pallas_call(
         cut_kernel,
+        grid=(part // chunk,),
         out_shape=(
             jax.ShapeDtypeStruct((part, 3 * slots * part), bf16),
-            jax.ShapeDtypeStruct((2 * part, slots * part), bf16),
+            jax.ShapeDtypeStruct((2, part, slots * part), bf16),
         ),
-        in_specs=[SM, VM],
-        out_specs=(VM, VM),
-        scratch_shapes=[pltpu.VMEM((part, wide // part * lane_block(part)), bf16)],
+        in_specs=[pl.BlockSpec((slots, chunk, wide), lambda i: (0, i, 0))],
+        out_specs=(
+            pl.BlockSpec((chunk, 3 * slots * part), lambda i: (i, 0)),
+            pl.BlockSpec((2, chunk, slots * part), lambda i: (0, i, 0)),
+        ),
+        scratch_shapes=[pltpu.VMEM((chunk, wide // part * lane_block(part)), bf16)],
         compiler_params=params(WHOLE),
         cost_estimate=cost(0, 8 * rows.size),
         name="cut",
-    )(pos, rows)
-
-
-def patch_kernel(shards, s, pos_ref, rows_ref, plus_ref, minus_ref, far_ref, out_hbm, out_ref, sem):
+    )(rows)
+    return plus, minus.reshape(2 * part, slots * part)
+
+
+def patch_kernel(shards, s, rows_ref, plus_ref, minus_ref, far_ref, out_hbm, out_ref, sem):
     part, wide = rows_ref.shape[1:]
     count = wide // part
     gap = out_ref.shape[1] // count
     each = wide // shards
-    pos = pos_ref[0]
+    pos = position()
     row = lax.broadcasted_iota(jnp.int32, (part, gap), 0)
     col = lax.broadcasted_iota(jnp.int32, (part, gap), 1)
     place = (col == (row // each) * lifted(each) + lax.rem(row, each)).astype(f32).astype(bf16)
@@ -261,7 +291,7 @@
     return (n + 7) // 8 * 8
 
 
-def patch(slot, pos, shards, rows, plus, minus, far):
+def patch(slot, shards, rows, plus, minus, far):
     _, part, wide = rows.shape
     count = wide // part
     gap = lane_block(shards // count * lifted(wide // shards))
@@ -275,7 +305,6 @@
         grid=(1,),
         out_shape=jax.ShapeDtypeStruct(shape, bf16),
         in_specs=[
-            SM,
             pl.BlockSpec((1, part, wide), lambda n: (slot, 0, 0)),
             whole(plus),
             whole(minus),
@@ -285,7 +314,7 @@
         scratch_shapes=[pltpu.VMEM(shape, bf16), pltpu.SemaphoreType.DMA],
         compiler_params=params(24),
         cost_estimate=cost(wide * wide * part, 3 * wide * wide),
-    )(pos, rows, plus, minus, far)
+    )(rows, plus, minus, far)
 
 
 def spread(pos, count, parts, full_ref, sems):
@@ -307,25 +336,39 @@
 
 
 def precond_kernel(count, shards, slot, *refs):
-    pos_ref, right_ref, adam_ref, root_ref = refs[:4]
-    grads = refs[4:8]
-    out_hbm = refs[8]
-    full_ref, root_buf, right_buf, prod_ref, pre_ref, out_ref, sems = refs[9:]
-    first = spread(pos_ref[0], count, grads, full_ref, sems)
-    first.append(pltpu.make_async_copy(right_ref.at[slot], right_buf, sems.at[4]))
-    second = pltpu.make_async_copy(root_ref, root_buf, sems.at[5])
-    for c in first:
+    right_ref, adam_ref, root_ref = refs[:3]
+    grads = refs[3:7]
+    out_hbm = refs[7]
+    full_ref, root_buf, right_buf, adam_buf, prod_ref, pre_ref, out_ref, sems = refs[8:]
+    part, wide = right_buf.shape
+    gap = root_buf.shape[1] // count
+    step = wide // 3
+    first = pltpu.make_async_copy(right_ref.at[slot], right_buf, sems.at[3, 0])
+    second = pltpu.make_async_copy(root_ref, root_buf, sems.at[3, 1])
+    third = pltpu.make_async_copy(adam_ref, adam_buf, sems.at[3, 2])
+    chunks = [
+        spread(
+            position(),
+            count,
+            [g.at[:, pl.ds(n * step, step)] for g in grads],
+            full_ref.at[:, pl.ds(n * step, step)],
+            sems.at[n],
+        )
+        for n in range(3)
+    ]
+    first.start()
+    for c in sum(chunks, []):
         c.start()
     second.start()
-    part, wide = right_buf.shape
-    gap = root_buf.shape[1] // count
-    for c in first:
-        c.wait()
-    step = wide // 3
+    third.start()
+    first.wait()
     for n in range(3):
         cols = slice(n * step, (n + 1) * step)
+        for c in chunks[n]:
+            c.wait()
         prod_ref[:, cols] = dot(right_buf[...], full_ref[:, cols], NN).astype(bf16)
     second.wait()
+    third.wait()
     total = jnp.zeros((1, 1), f32)
     for k in range(count):
         got = dot(prod_ref[...], root_buf[:, k * gap : (k + 1) * gap], NN)
@@ -333,49 +376,57 @@
         total = total + jnp.sum(got * got, keepdims=True)
     lane = lax.broadcasted_iota(jnp.int32, (8, 128), 1)
     extra = jnp.zeros((8, 128), f32)
-    for i, value in enumerate(pieces_of(total) + pieces_of(adam_ref[0:1, 0:1])):
+    for i, value in enumerate(pieces_of(total) + pieces_of(adam_buf[0:1, 0:1])):
         extra = jnp.where(lane == 32 + i, value, extra)
     lift = lifted(wide // shards)
     blank = jnp.zeros((lane_block(part) - part, gap), f32)
+    per = shards // count
+    sent = [
+        pltpu.make_async_copy(
+            out_ref.at[pl.ds(k * per, per)], out_hbm.at[pl.ds(k * per, per)], sems.at[4, k]
+        )
+        for k in range(count)
+    ]
     for k in range(count):
         turned = jnp.concatenate([pre_ref[k], blank], axis=0).T
         for j in range(shards // count):
             block = pack(turned[j * lift : (j + 1) * lift], extra)
             out_ref[k * (shards // count) + j] = block.astype(bf16)
-    last = pltpu.make_async_copy(out_ref, out_hbm, sems.at[0])
-    last.start()
-    last.wait()
-
-
-def precondition(pos, count, shards, slot, right, adam, root, grads):
+        sent[k].start()
+    for c in sent:
+        c.wait()
+
+
+def precondition(count, shards, slot, right, adam, root, grads):
     part, wide = grads[0].shape
     long = root.shape[1]
     gap = long // count
     return pl.pallas_call(
         lambda *refs: precond_kernel(count, shards, slot, *refs),
         out_shape=jax.ShapeDtypeStruct((shards, PACKED, 128), bf16),
-        in_specs=[SM, HB, VM, HB] + [HB] * 4,
+        in_specs=[HB] * 7,
         out_specs=HB,
         scratch_shapes=[
             pltpu.VMEM((wide, wide), bf16),
             pltpu.VMEM((wide, long), bf16),
             pltpu.VMEM((part, wide), bf16),
+            pltpu.VMEM((8, 128), f32),
             pltpu.VMEM((part, wide), bf16),
             pltpu.VMEM((count, part, gap), f32),
             pltpu.VMEM((shards, PACKED, 128), bf16),
-            pltpu.SemaphoreType.DMA((6,)),
+            pltpu.SemaphoreType.DMA((5, count)),
         ],
         compiler_params=params(WHOLE),
         cost_estimate=cost(4 * part * wide * wide, 4 * wide * wide),
-    )(pos, right, adam, root, *grads)
+    )(right, adam, root, *grads)
 
 
 def gram_kernel(count, slot, *refs):
-    pos_ref, left_ref, right_ref = refs[:3]
-    grads = refs[3:7]
-    outl_ref, outr_ref, full_ref, own_ref, sems = refs[7 + 2 * slot :]
+    left_ref, right_ref = refs[:2]
+    grads = refs[2:6]
+    outl_ref, outr_ref, full_ref, own_ref, sems = refs[6 + 2 * slot :]
     n = pl.program_id(0)
-    pos = pos_ref[0]
+    pos = position()
     wide = full_ref.shape[1]
     part = own_ref.shape[1]
     step = outl_ref.shape[2]
@@ -401,7 +452,7 @@
     outr_ref[0] = stat_decay * right_ref[0] + right / wide
 
 
-def grams(pos, count, slot, left, right, grads, before=()):
+def grams(count, slot, left, right, grads, before=()):
     _, part, wide = left.shape
     step = wide // 3
     block = pl.BlockSpec((1, part, step), lambda n: (slot, 0, n))
@@ -410,17 +461,17 @@
         lambda *refs: gram_kernel(count, slot, *refs),
         grid=(3,),
         out_shape=(shape, shape),
-        in_specs=[SM, block, block] + [HB] * (4 + len(before)),
+        in_specs=[block, block] + [HB] * (4 + len(before)),
         out_specs=(block, block),
         scratch_shapes=[
             pltpu.VMEM((wide, wide), bf16),
             pltpu.VMEM((wide, part), bf16),
             pltpu.SemaphoreType.DMA((4,)),
         ],
-        input_output_aliases={7 + i: i for i in range(len(before))},
+        input_output_aliases={6 + i: i for i in range(len(before))},
         compiler_params=params(WHOLE),
         cost_estimate=cost(4 * part * wide * wide, 20 * part * wide),
-    )(pos, left, right, *grads, *before)
+    )(left, right, *grads, *before)
 
 
 def sums_kernel(back0_ref, back1_ref, out_ref):
@@ -521,7 +572,6 @@
 def step(gradients, weights, owner_list, left_stats, right_stats, left_root, right_root, moment):
     shards = lax.axis_size("shard")
     count = lax.axis_size("tensor")
-    pos = lax.axis_index("tensor").astype(jnp.int32).reshape(1)
 
     def shift(x, by):
         ring = [(i, (i + by) % count) for i in range(count)]
@@ -536,7 +586,7 @@
     mom_rows = jnp.swapaxes(moment, 1, 2)
     part, wide = left_rows.shape[1:]
 
-    plus, minus = cut(pos, left_rows)
+    plus, minus = cut(left_rows)
     plus, minus = shift(plus, 1), shift(minus, -1)
     far = shift(minus[:part], -1)
 
@@ -553,13 +603,13 @@
         new_moment, adam = moments(s, parts[s], mom_rows, before)
         before = (new_moment,)
         adams.append(adam)
-        roots.append(patch(s, pos, shards, left_rows, plus, minus, far))
+        roots.append(patch(s, shards, left_rows, plus, minus, far))
     for s in range(2):
-        update = precondition(pos, count, shards, s, right_rows, adams[s], roots[s], grads[s])
+        update = precondition(count, shards, s, right_rows, adams[s], roots[s], grads[s])
         backs.append(exchange(update))
     stats = ()
     for s in range(2):
-        stats = grams(pos, count, s, left_stats, right_stats, grads[s], stats)
+        stats = grams(count, s, left_stats, right_stats, grads[s], stats)
     new_left, new_right = stats
     mine = partial_sums(backs[0], backs[1])
 

time: 180 us -> 178 us (0.989)
  Pallas kernels: 59.8 us -> 56.9 us
  transfers between devices with their start and end apart: 14 -> 14, of which waited for: 5 -> 5; matrix products, arithmetic and copies ran while one was open for 0% -> 0% of each run, Pallas kernels for 30% -> 29%
where the time goes in v2:
time: 178 us; the launch traced here: 177 us
  Pallas kernels  56.9 us (32%)
  starting transfers between devices  42.5 us (24%)
  waiting for transfers between devices  38.4 us (22%)
  blocking collectives  21 us (12%)
  local copies, waits for them, and re-layouts  17 us (10%)
    ppermute x9, waiting for transfers between devices, shift(): return lax.ppermute(x, 'tensor', ring)  25.4 us
    all_to_all x3, starting transfers between devices, exchange(): return lax.all_to_all(x, 'shard', 0, 0, tiled=True)  21.9 us
    all_to_all x1, blocking collectives, exchange(): return lax.all_to_all(x, 'shard', 0, 0, tiled=True)  21 us
    ppermute x9, starting transfers between devices, shift(): return lax.ppermute(x, 'tensor', ring)  17.2 us
    unnamed x44, local copies, waits for them, and re-layouts  17 us
    pallas_call x2, Pallas kernels, grams(): pl.pallas_call(lambda *refs: gram_kernel(count, slot, *refs), grid=(3,),...  14.2 us
    all_to_all x3, waiting for transfers between devices, exchange(): return lax.all_to_all(x, 'shard', 0, 0, tiled=True)  13 us
    pallas_call x2, Pallas kernels, precondition(): pl.pallas_call(lambda *refs: precond_kernel(count, shards, slot, *refs),...  12 us
  transfers between devices with their start and end apart: 14, of which 5 were waited for; matrix products, arithmetic and copies ran while one was open for 0% of the time, Pallas kernels for 29%

profile of v2, /device:TPU:1, one launch (start us, length us, event | category | flops | bytes accessed | tf_op | source)
XLA Modules:
  0.0 176.6 jit_solution(12941749959608745900)
XLA Ops:
  0.6 3.8 %shard_map.115 = bf16[32,88,128]{2,1,0:T(8,128)(2,1)} custom-call(s32[32]{0:T(128)} %owner_ref.1, bf16[36,32,288]{2,1,0:T(8,128)(2,1)} %bitcast.16), custom_call_target="tpu_custom_call" | custom-call | bytes 1658880 | tf_op jit(solution)/shard_map/pallas_call | solution.py:120
  4.4 9.4 %all-to-all-start.2 = ((bf16[32,88,128]{2,1,0:T(8,128)(2,1)}), bf16[32,88,128]{2,1,0:T(8,128)(2,1)S(1)}, u32[]{:S(2)}, u32[]{:S(2)}) async-start(bf16[32,88,128]{2,1,0:T(8,128)(2,1)} %shard_map.115), calls=%async_computation.2 | async-start | bytes 1441792 | tf_op jit(solution)/shard_map/all_to_all | solution.py:581
  13.9 4.4 %shard_map.111 = bf16[32,88,128]{2,1,0:T(8,128)(2,1)} custom-call(s32[32]{0:T(128)} %owner_ref.1, bf16[36,32,288]{2,1,0:T(8,128)(2,1)} %bitcast.17), custom_call_target="tpu_custom_call" | custom-call | bytes 1658880 | tf_op jit(solution)/shard_map/pallas_call | solution.py:120
  18.3 9.1 %all-to-all-done.2.got_ref = bf16[32,88,128]{2,1,0:T(8,128)(2,1)S(1)} async-done(((bf16[32,88,128]{2,1,0:T(8,128)(2,1)}), bf16[32,88,128]{2,1,0:T(8,128)(2,1)S(1)}, u32[]{:S(2)}, u32[]{:S(2)}) %all-to-all-start.2) | async-done | bytes 720928 | tf_op jit(solution)/shard_map/all_to_all | solution.py:581
  27.4 0.9 copy-done.12
  28.3 4.4 %all-to-all-start = ((bf16[32,88,128]{2,1,0:T(8,128)(2,1)}), bf16[32,88,128]{2,1,0:T(8,128)(2,1)}, u32[]{:S(2)}, u32[]{:S(2)}) async-start(bf16[32,88,128]{2,1,0:T(8,128)(2,1)} %shard_map.111), calls=%async_computation | async-start | bytes 1441792 | tf_op jit(solution)/shard_map/all_to_all | solution.py:581
  32.7 1.1 copy-done.13
  33.8 0.6 turn.3.refs_0_.refs_3_.refs_2_
  34.4 2.8 %collective-permute-start.7 = (bf16[288,1152]{1,0:T(8,128)(2,1)S(1)}, bf16[288,1152]{1,0:T(8,128)(2,1)}, u32[]{:S(2)}, u32[]{:S(2)}) collective-permute-start(bf16[288,1152]{1,0:T(8,128)(2,1)S(1)} %turn.3.refs_0_.refs_3_.refs_2_), channel_id=1, source_target_pairs={{0,3},{1,0},{2,1},{3,2},{4,7},{5,4},{6,5},{7,6},{8,11},{9,8},{10,9... | collective-permute-start | bytes 1990664 | tf_op jit(solution)/shard_map/ppermute | solution.py:578
  37.2 3.6 %cut.1 = (bf16[288,1728]{1,0:T(8,128)(2,1)}, bf16[2,288,576]{2,1,0:T(8,128)(2,1)}) custom-call(bf16[2,288,1152]{2,1,0:T(8,128)(2,1)} %bitcast.8), custom_call_target="tpu_custom_call" | custom-call | bytes 5308416 | tf_op jit(solution)/shard_map/cut/pallas_call | solution.py:231
  40.8 0.4 collective-permute-start.1
  41.3 1.0 collective-permute-start
  42.3 3.9 %all-to-all-done.got_ref = bf16[32,88,128]{2,1,0:T(8,128)(2,1)} async-done(((bf16[32,88,128]{2,1,0:T(8,128)(2,1)}), bf16[32,88,128]{2,1,0:T(8,128)(2,1)}, u32[]{:S(2)}, u32[]{:S(2)}) %all-to-all-start) | async-done | bytes 720928 | tf_op jit(solution)/shard_map/all_to_all | solution.py:581
  46.1 2.3 %turn.2.refs_0_.refs_3_.refs_2_ = bf16[288,1152]{1,0:T(8,128)(2,1)} custom-call(bf16[32,88,128]{2,1,0:T(8,128)(2,1)} %all-to-all-done.got_ref), custom_call_target="tpu_custom_call" | custom-call | bytes 1802240 | tf_op jit(solution)/shard_map/turn/pallas_call | solution.py:154
  48.5 1.4 collective-permute-start.3
  49.9 1.3 collective-permute-start.6
  51.2 0.2 collective-permute-done.7.refs_5_.refs_4_
  51.4 3.5 %collective-permute-start.8 = (bf16[288,1152]{1,0:T(8,128)(2,1)}, bf16[288,1152]{1,0:T(8,128)(2,1)S(1)}, u32[]{:S(2)}, u32[]{:S(2)}) collective-permute-start(bf16[288,1152]{1,0:T(8,128)(2,1)} %collective-permute-done.7.refs_5_.refs_4_), channel_id=1, source_target_pairs={{0,3},{1,0},{2,1},{3,2},{4,7},{5,4},{6,5},{7,6},{8,11},{9,8},{10,9... | collective-permute-start | bytes 1990664 | tf_op jit(solution)/shard_map/ppermute | solution.py:578
  54.9 12.4 %collective-permute-done.1.refs_2_ = bf16[576,576]{1,0:T(8,128)(2,1)S(1)} collective-permute-done((bf16[576,576]{1,0:T(8,128)(2,1)}, bf16[576,576]{1,0:T(8,128)(2,1)S(1)}, u32[]{:S(2)}, u32[]{:S(2)}) %collective-permute-start.1) | collective-permute-done | bytes 663584 | tf_op jit(solution)/shard_map/ppermute | solution.py:578
  67.3 3.4 %collective-permute-start.2 = (bf16[288,576]{1,0:T(8,128)(2,1)S(1)}, bf16[288,576]{1,0:T(8,128)(2,1)S(1)}, u32[]{:S(2)}, u32[]{:S(2)}) collective-permute-start(bf16[288,576]{1,0:T(8,128)(2,1)S(1)} %slice.4), channel_id=1, source_target_pairs={{0,3},{1,0},{2,1},{3,2},{4,7},{5,4},{6,5},{7,6},{8,11},{9,8},{10,9... | collective-permute-start | bytes 995336 | tf_op jit(solution)/shard_map/ppermute | solution.py:578
  70.7 1.7 copy-done.5
  72.5 2.6 %shard_map.112 = (f32[2,288,1152]{2,1,0:T(8,128)}, f32[8,128]{1,0:T(8,128)S(1)}) custom-call(bf16[288,1152]{1,0:T(8,128)(2,1)} %turn.2.refs_0_.refs_3_.refs_2_, f32[2,288,1152]{2,1,0:T(8,128)S(1)} %bitcast.11), custom_call_target="tpu_custom_call" | custom-call | flops 3317760 | bytes 3317760 | tf_op jit(solution)/shard_map/pallas_call | solution.py:182
  75.1 1.5 shard_map.116
  76.6 12.7 %collective-permute-done.2.refs_3_ = bf16[288,576]{1,0:T(8,128)(2,1)S(1)} collective-permute-done((bf16[288,576]{1,0:T(8,128)(2,1)S(1)}, bf16[288,576]{1,0:T(8,128)(2,1)S(1)}, u32[]{:S(2)}, u32[]{:S(2)}) %collective-permute-start.2) | collective-permute-done | bytes 331808 | tf_op jit(solution)/shard_map/ppermute | solution.py:578
  89.3 3.4 %collective-permute-start.4 = (bf16[288,1152]{1,0:T(8,128)(2,1)}, bf16[288,1152]{1,0:T(8,128)(2,1)}, u32[]{:S(2)}, u32[]{:S(2)}) collective-permute-start(bf16[288,1152]{1,0:T(8,128)(2,1)} %turn.2.refs_0_.refs_3_.refs_2_), channel_id=1, source_target_pairs={{0,3},{1,0},{2,1},{3,2},{4,7},{5,4},{6,5},{7,6},{8,11},{9,8},{10,9... | collective-permute-start | bytes 1990664 | tf_op jit(solution)/shard_map/ppermute | solution.py:578
  92.8 2.9 %shard_map.117.refs_2_ = bf16[1152,1536]{1,0:T(8,128)(2,1)S(1)} custom-call(bf16[2,288,1152]{2,1,0:T(8,128)(2,1)S(1)} %bitcast.9, bf16[288,1728]{1,0:T(8,128)(2,1)S(1)} %collective-permute-done.refs_1_, bf16[576,576]{1,0:T(8,128)(2,1)S(1)} %collective-permute-done.1.refs_2_, bf16[288,576]{1,0:T(8,128)(2,1)S(1)} %collective-permute-done.2.refs_3_), custom_call_target="tpu_custom_call" | custom-call | flops 382205952 | bytes 3981312 | tf_op jit(solution)/shard_map/pallas_call | solution.py:303
  95.7 1.7 copy-done
  97.5 0.8 copy-done.20
  98.3 0.9 copy-done.21
  99.2 6.0 %shard_map.118 = bf16[32,88,128]{2,1,0:T(8,128)(2,1)} custom-call(bf16[2,288,1152]{2,1,0:T(8,128)(2,1)} %bitcast.14, f32[8,128]{1,0:T(8,128)} %copy-done.19, bf16[1152,1536]{1,0:T(8,128)(2,1)} %copy-done, bf16[288,1152]{1,0:T(8,128)(2,1)} %copy-done.4, bf16[288,1152]{1,0:T(8,128)(2,1)} %copy-done.20, ...), custom_call_target="tpu_custom_call" | custom-call | flops 1528823808 | bytes 5308416 | tf_op jit(solution)/shard_map/pallas_call | solution.py:404
  105.2 8.1 %all-to-all-start.3 = ((bf16[32,88,128]{2,1,0:T(8,128)(2,1)}), bf16[32,88,128]{2,1,0:T(8,128)(2,1)S(1)}, u32[]{:S(2)}, u32[]{:S(2)}) async-start(bf16[32,88,128]{2,1,0:T(8,128)(2,1)} %shard_map.118), calls=%async_computation.3 | async-start | bytes 1441792 | tf_op jit(solution)/shard_map/all_to_all | solution.py:581
  113.3 1.3 copy-done.3
  114.6 1.1 copy-done.9
  115.7 1.2 copy-done.11
  116.9 1.0 copy-done.16
  117.9 2.9 %shard_map.113.refs_2_ = bf16[1152,1536]{1,0:T(8,128)(2,1)S(1)} custom-call(bf16[2,288,1152]{2,1,0:T(8,128)(2,1)S(1)} %bitcast.10, bf16[288,1728]{1,0:T(8,128)(2,1)S(1)} %copy-done.11, bf16[576,576]{1,0:T(8,128)(2,1)S(1)} %copy-done.9, bf16[288,576]{1,0:T(8,128)(2,1)S(1)} %copy-done.16), custom_call_target="tpu_custom_call" | custom-call | flops 382205952 | bytes 3981312 | tf_op jit(solution)/shard_map/pallas_call | solution.py:303
  120.9 1.7 copy-done.1
  122.6 6.0 %shard_map.114 = bf16[32,88,128]{2,1,0:T(8,128)(2,1)} custom-call(bf16[2,288,1152]{2,1,0:T(8,128)(2,1)} %bitcast.15, f32[8,128]{1,0:T(8,128)} %copy-done.18, bf16[1152,1536]{1,0:T(8,128)(2,1)} %copy-done.1, bf16[288,1152]{1,0:T(8,128)(2,1)} %turn.2.refs_0_.refs_3_.refs_2_, bf16[288,1152]{1,0:T(8,128)(2,1)} %collective-permute-done.3.refs_4_.refs_3_, ...), custom_call_target="tpu_custom_call" | custom-call | flops 1528823808 | bytes 5308416 | tf_op jit(solution)/shard_map/pallas_call | solution.py:404
  128.6 21.0 %all_to_all.20.back0_ref = bf16[32,88,128]{2,1,0:T(8,128)(2,1)S(1)} all-to-all(bf16[32,88,128]{2,1,0:T(8,128)(2,1)} %shard_map.114), channel_id=1, replica_groups=mesh['shard'=32,'tensor'=4] {'shard'}, dimensions={0} | all-to-all | bytes 1441792 | tf_op jit(solution)/shard_map/all_to_all | solution.py:581
  149.6 0.5 sums.1
  150.1 0.9 copy-done.6
  150.9 7.1 %shard_map.119 = (f32[2,288,1152]{2,1,0:T(8,128)}, f32[2,288,1152]{2,1,0:T(8,128)}) custom-call(f32[2,288,1152]{2,1,0:T(8,128)} %refs_0_.7, f32[2,288,1152]{2,1,0:T(8,128)} %refs_1_.3, bf16[288,1152]{1,0:T(8,128)(2,1)} %turn.2.refs_0_.refs_3_.refs_2_, bf16[288,1152]{1,0:T(8,128)(2,1)} %collective-permute-done.3.refs_4_.refs_3_, ...), custom_call_target="tpu_custom_call" | custom-call | flops 1528823808 | bytes 6635520 | tf_op jit(solution)/shard_map/pallas_call | solution.py:460
  158.0 3.4 %collective-permute-start.10 = (f32[8,128]{1,0:T(8,128)S(1)}, f32[8,128]{1,0:T(8,128)S(1)}, u32[]{:S(2)}, u32[]{:S(2)}) collective-permute-start(f32[8,128]{1,0:T(8,128)S(1)} %add.3.refs_0_), channel_id=1, source_target_pairs={{0,3},{1,2},{2,1},{3,0},{4,7},{5,6},{6,5},{7,4},{8,11},{9,10},{10,... | collective-permute-start | bytes 12296 | tf_op jit(solution)/shard_map/ppermute | solution.py:618
  161.4 7.1 %shard_map.120 = (f32[2,288,1152]{2,1,0:T(8,128)}, f32[2,288,1152]{2,1,0:T(8,128)}) custom-call(f32[2,288,1152]{2,1,0:T(8,128)} %refs_0_.7, f32[2,288,1152]{2,1,0:T(8,128)} %refs_1_.3, bf16[288,1152]{1,0:T(8,128)(2,1)} %copy-done.4, bf16[288,1152]{1,0:T(8,128)(2,1)} %copy-done.20, ...), custom_call_target="tpu_custom_call", output_to_operand_aliasing={{0}: (6, {}), {1}: (7, {})} | custom-call | flops 1528823808 | bytes 6635520 | tf_op jit(solution)/shard_map/pallas_call | solution.py:460
  168.5 1.1 copy-done.7
  169.6 4.1 %place.1 = (f32[36,32,288]{2,1,0:T(8,128)S(1)}, f32[2,32,128]{2,1,0:T(8,128)S(1)}) custom-call(s32[32]{0:T(128)S(1)} %copy-done.17, bf16[32,88,128]{2,1,0:T(8,128)(2,1)S(1)} %copy-done.7, bf16[32,88,128]{2,1,0:T(8,128)(2,1)S(1)} %all-to-all-done.3.back1_ref), custom_call_target="tpu_custom_call" | custom-call | bytes 2654208 | tf_op jit(solution)/shard_map/place/pallas_call | solution.py:530
  173.7 1.5 copy-done.14
  175.2 1.5 final.1
  (43 shorter events, 0.1 us)
Async XLA Ops:
  4.4 23.0 %all-to-all-start.2 = ((bf16[32,88,128]{2,1,0:T(8,128)(2,1)}), bf16[32,88,128]{2,1,0:T(8,128)(2,1)S(1)}, u32[]{:S(2)}, u32[]{:S(2)}) async-start(bf16[32,88,128]{2,1,0:T(8,128)(2,1)} %shard_map.115), calls=%async_computation.2 | async-start | bytes 1441792 | tf_op jit(solution)/shard_map/all_to_all | solution.py:581
  27.4 0.9 copy-start.12
  28.3 17.9 %all-to-all-start = ((bf16[32,88,128]{2,1,0:T(8,128)(2,1)}), bf16[32,88,128]{2,1,0:T(8,128)(2,1)}, u32[]{:S(2)}, u32[]{:S(2)}) async-start(bf16[32,88,128]{2,1,0:T(8,128)(2,1)} %shard_map.111), calls=%async_computation | async-start | bytes 1441792 | tf_op jit(solution)/shard_map/all_to_all | solution.py:581
  32.7 1.1 copy-start.13
  34.4 40.7 %copy-start.4 = (bf16[288,1152]{1,0:T(8,128)(2,1)}, bf16[288,1152]{1,0:T(8,128)(2,1)S(1)}, u32[]{:S(2)}) copy-start(bf16[288,1152]{1,0:T(8,128)(2,1)S(1)} %turn.3.refs_0_.refs_3_.refs_2_) | copy-start | bytes 1990660
  34.4 17.0 %collective-permute-start.7 = (bf16[288,1152]{1,0:T(8,128)(2,1)S(1)}, bf16[288,1152]{1,0:T(8,128)(2,1)}, u32[]{:S(2)}, u32[]{:S(2)}) collective-permute-start(bf16[288,1152]{1,0:T(8,128)(2,1)S(1)} %turn.3.refs_0_.refs_3_.refs_2_), channel_id=1, source_target_pairs={{0,3},{1,0},{2,1},{3,2},{4,7},{5,4},{6,5},{7,6},{8,11},{9,8},{10,9... | collective-permute-start | bytes 1990664 | tf_op jit(solution)/shard_map/ppermute | solution.py:578
  40.8 26.5 %collective-permute-start.1 = (bf16[576,576]{1,0:T(8,128)(2,1)}, bf16[576,576]{1,0:T(8,128)(2,1)S(1)}, u32[]{:S(2)}, u32[]{:S(2)}) collective-permute-start(bf16[576,576]{1,0:T(8,128)(2,1)} %bitcast.20), channel_id=1, source_target_pairs={{0,3},{1,0},{2,1},{3,2},{4,7},{5,4},{6,5},{7,6},{8,11},{9,8},{10,9... | collective-permute-start | bytes 1990664 | tf_op jit(solution)/shard_map/ppermute | solution.py:578
  41.3 51.5 %collective-permute-start = (bf16[288,1728]{1,0:T(8,128)(2,1)}, bf16[288,1728]{1,0:T(8,128)(2,1)S(1)}, u32[]{:S(2)}, u32[]{:S(2)}) collective-permute-start(bf16[288,1728]{1,0:T(8,128)(2,1)} %get-tuple-element.17), channel_id=1, source_target_pairs={{0,1},{1,2},{2,3},{3,0},{4,5},{5,6},{6,7},{7,4},{8,9},{9,10},{10,1... | collective-permute-start | bytes 2985992 | tf_op jit(solution)/shard_map/ppermute | solution.py:578
  48.5 49.0 %collective-permute-start.3 = (bf16[288,1152]{1,0:T(8,128)(2,1)}, bf16[288,1152]{1,0:T(8,128)(2,1)}, u32[]{:S(2)}, u32[]{:S(2)}) collective-permute-start(bf16[288,1152]{1,0:T(8,128)(2,1)} %turn.2.refs_0_.refs_3_.refs_2_), channel_id=1, source_target_pairs={{0,1},{1,2},{2,3},{3,0},{4,5},{5,6},{6,7},{7,4},{8,9},{9,10},{10,1... | collective-permute-start | bytes 1990664 | tf_op jit(solution)/shard_map/ppermute | solution.py:578
  49.9 47.6 %collective-permute-start.6 = (bf16[288,1152]{1,0:T(8,128)(2,1)S(1)}, bf16[288,1152]{1,0:T(8,128)(2,1)S(1)}, u32[]{:S(2)}, u32[]{:S(2)}) collective-permute-start(bf16[288,1152]{1,0:T(8,128)(2,1)S(1)} %turn.3.refs_0_.refs_3_.refs_2_), channel_id=1, source_target_pairs={{0,1},{1,2},{2,3},{3,0},{4,5},{5,6},{6,7},{7,4},{8,9},{9,10},{10,1... | collective-permute-start | bytes 1990664 | tf_op jit(solution)/shard_map/ppermute | solution.py:578
  51.4 46.9 %collective-permute-start.8 = (bf16[288,1152]{1,0:T(8,128)(2,1)}, bf16[288,1152]{1,0:T(8,128)(2,1)S(1)}, u32[]{:S(2)}, u32[]{:S(2)}) collective-permute-start(bf16[288,1152]{1,0:T(8,128)(2,1)} %collective-permute-done.7.refs_5_.refs_4_), channel_id=1, source_target_pairs={{0,3},{1,0},{2,1},{3,2},{4,7},{5,4},{6,5},{7,6},{8,11},{9,8},{10,9... | collective-permute-start | bytes 1990664 | tf_op jit(solution)/shard_map/ppermute | solution.py:578
  67.3 25.4 %copy-start.8 = (bf16[576,576]{1,0:T(8,128)(2,1)}, bf16[576,576]{1,0:T(8,128)(2,1)S(1)}, u32[]{:S(2)}) copy-start(bf16[576,576]{1,0:T(8,128)(2,1)S(1)} %collective-permute-done.1.refs_2_) | copy-start | bytes 1990660
  67.3 22.0 %collective-permute-start.2 = (bf16[288,576]{1,0:T(8,128)(2,1)S(1)}, bf16[288,576]{1,0:T(8,128)(2,1)S(1)}, u32[]{:S(2)}, u32[]{:S(2)}) collective-permute-start(bf16[288,576]{1,0:T(8,128)(2,1)S(1)} %slice.4), channel_id=1, source_target_pairs={{0,3},{1,0},{2,1},{3,2},{4,7},{5,4},{6,5},{7,6},{8,11},{9,8},{10,9... | collective-permute-start | bytes 995336 | tf_op jit(solution)/shard_map/ppermute | solution.py:578
  70.7 1.7 copy-start.5
  75.1 1.5 copy-start.18
  75.1 17.7 %copy-start.2 = (bf16[2,1152,288]{1,2,0:T(8,128)(2,1)S(1)}, bf16[2,1152,288]{1,2,0:T(8,128)(2,1)}, u32[]{:S(2)}) copy-start(bf16[2,1152,288]{1,2,0:T(8,128)(2,1)} %param.13) | copy-start | bytes 3981316
  76.6 19.1 %copy-start.19 = (f32[8,128]{1,0:T(8,128)}, f32[8,128]{1,0:T(8,128)S(1)}, u32[]{:S(2)}) copy-start(f32[8,128]{1,0:T(8,128)S(1)} %get-tuple-element.20.refs_1_) | copy-start | bytes 12292
  89.3 6.4 %copy-start.15 = (bf16[288,576]{1,0:T(8,128)(2,1)}, bf16[288,576]{1,0:T(8,128)(2,1)S(1)}, u32[]{:S(2)}) copy-start(bf16[288,576]{1,0:T(8,128)(2,1)S(1)} %collective-permute-done.2.refs_3_) | copy-start | bytes 995332
  89.3 33.3 %collective-permute-start.4 = (bf16[288,1152]{1,0:T(8,128)(2,1)}, bf16[288,1152]{1,0:T(8,128)(2,1)}, u32[]{:S(2)}, u32[]{:S(2)}) collective-permute-start(bf16[288,1152]{1,0:T(8,128)(2,1)} %turn.2.refs_0_.refs_3_.refs_2_), channel_id=1, source_target_pairs={{0,3},{1,0},{2,1},{3,2},{4,7},{5,4},{6,5},{7,6},{8,11},{9,8},{10,9... | collective-permute-start | bytes 1990664 | tf_op jit(solution)/shard_map/ppermute | solution.py:578
  92.7 3.0 %copy-start.10 = (bf16[288,1728]{1,0:T(8,128)(2,1)}, bf16[288,1728]{1,0:T(8,128)(2,1)S(1)}, u32[]{:S(2)}) copy-start(bf16[288,1728]{1,0:T(8,128)(2,1)S(1)} %collective-permute-done.refs_1_) | copy-start | bytes 2985988
  95.7 1.7 copy-start
  97.5 25.1 %collective-permute-start.5 = (bf16[288,1152]{1,0:T(8,128)(2,1)}, bf16[288,1152]{1,0:T(8,128)(2,1)}, u32[]{:S(2)}, u32[]{:S(2)}) collective-permute-start(bf16[288,1152]{1,0:T(8,128)(2,1)} %collective-permute-done.3.refs_4_.refs_3_), channel_id=1, source_target_pairs={{0,1},{1,2},{2,3},{3,0},{4,5},{5,6},{6,7},{7,4},{8,9},{9,10},{10,1... | collective-permute-start | bytes 1990664 | tf_op jit(solution)/shard_map/ppermute | solution.py:578
  97.5 0.8 copy-start.20
  98.3 0.9 copy-start.21
  105.2 23.4 %all-to-all-start.3 = ((bf16[32,88,128]{2,1,0:T(8,128)(2,1)}), bf16[32,88,128]{2,1,0:T(8,128)(2,1)S(1)}, u32[]{:S(2)}, u32[]{:S(2)}) async-start(bf16[32,88,128]{2,1,0:T(8,128)(2,1)} %shard_map.118), calls=%async_computation.3 | async-start | bytes 1441792 | tf_op jit(solution)/shard_map/all_to_all | solution.py:581
  113.3 1.3 copy-start.3
  114.6 1.1 copy-start.9
  115.7 1.2 copy-start.11
  116.9 1.0 copy-start.16
  120.8 1.7 copy-start.1
  150.1 0.9 copy-start.6
  150.9 7.1 %collective-permute-start.9 = (f32[8,128]{1,0:T(8,128)S(1)}, f32[8,128]{1,0:T(8,128)S(1)}, u32[]{:S(2)}, u32[]{:S(2)}) collective-permute-start(f32[8,128]{1,0:T(8,128)S(1)} %sums.1), channel_id=1, source_target_pairs={{0,1},{1,0},{2,3},{3,2},{4,5},{5,4},{6,7},{7,6},{8,9},{9,8},{10,11... | collective-permute-start | bytes 12296 | tf_op jit(solution)/shard_map/ppermute | solution.py:618
  158.0 15.6 %collective-permute-start.10 = (f32[8,128]{1,0:T(8,128)S(1)}, f32[8,128]{1,0:T(8,128)S(1)}, u32[]{:S(2)}, u32[]{:S(2)}) collective-permute-start(f32[8,128]{1,0:T(8,128)S(1)} %add.3.refs_0_), channel_id=1, source_target_pairs={{0,3},{1,2},{2,1},{3,0},{4,7},{5,6},{6,5},{7,4},{8,11},{9,10},{10,... | collective-permute-start | bytes 12296 | tf_op jit(solution)/shard_map/ppermute | solution.py:618
  161.4 7.1 %copy-start.17 = (s32[32]{0:T(128)S(1)}, s32[32]{0:T(128)}, u32[]{:S(2)}) copy-start(s32[32]{0:T(128)} %owner_ref.1) | copy-start | bytes 388
  168.5 1.1 copy-start.7
  173.7 1.5 copy-start.14

commit v3 on v2

--- a/solution.py
+++ b/solution.py
@@ -134,7 +134,7 @@
     )(owner_list, gradients)
 
 
-def turn_kernel(got_ref, out_hbm, wide_ref, out_ref, sem):
+def turn_kernel(got_ref, out_ref, wide_ref):
     count = got_ref.shape[0]
     rows = wide_ref.shape[0] // count
     for s in range(count):
@@ -145,8 +145,6 @@
 
         unpack(got_ref[s].astype(f32), put)
     out_ref[...] = wide_ref[...].T.astype(bf16)
-    pltpu.make_async_copy(out_ref, out_hbm, sem).start()
-    pltpu.make_async_copy(out_ref, out_hbm, sem).wait()
 
 
 def turn(got, rows, width):
@@ -155,12 +153,8 @@
         turn_kernel,
         out_shape=jax.ShapeDtypeStruct((width, count * rows), bf16),
         in_specs=[VM],
-        out_specs=HB,
-        scratch_shapes=[
-            pltpu.VMEM((count * rows, width), f32),
-            pltpu.VMEM((width, count * rows), bf16),
-            pltpu.SemaphoreType.DMA,
-        ],
+        out_specs=VM,
+        scratch_shapes=[pltpu.VMEM((count * rows, width), f32)],
         compiler_params=params(8),
         cost_estimate=cost(0, 5 * got.size),
         name="turn",
@@ -312,7 +306,7 @@
         ],
         out_specs=HB,
         scratch_shapes=[pltpu.VMEM(shape, bf16), pltpu.SemaphoreType.DMA],
-        compiler_params=params(24),
+        compiler_params=params(WHOLE),
         cost_estimate=cost(wide * wide * part, 3 * wide * wide),
     )(rows, plus, minus, far)
 

time: 178 us -> 175 us (0.983)
  local copies, waits for them, and re-layouts: 17 us -> 9.13 us
  Pallas kernels: 56.9 us -> 62.8 us
    unnamed x44 -> x24, local copies, waits for them, and re-layouts: 17 us -> 9.1 us
    pallas_call x2, Pallas kernels: 5.85 us -> 11.9 us  [patch(): pl.pallas_call(lambda *refs: patch_kernel(shards, slot, *refs), grid=(1,)...]
    all_to_all x3, waiting for transfers between devices: 13 us -> 14.8 us  [exchange(): return lax.all_to_all(x, 'shard', 0, 0, tiled=True)]
  transfers between devices with their start and end apart: 14 -> 14, of which waited for: 5 -> 5; matrix products, arithmetic and copies ran while one was open for 0% -> 0% of each run, Pallas kernels for 29% -> 33%
where the time goes in v3:
time: 175 us; the launch traced here: 174 us
  Pallas kernels  62.8 us (36%)
  starting transfers between devices  42.7 us (24%)
  waiting for transfers between devices  38.7 us (22%)
  blocking collectives  19.4 us (11%)
  local copies, waits for them, and re-layouts  9.13 us (5%)
    ppermute x9, waiting for transfers between devices, shift(): return lax.ppermute(x, 'tensor', ring)  24 us
    all_to_all x3, starting transfers between devices, exchange(): return lax.all_to_all(x, 'shard', 0, 0, tiled=True)  21.9 us
    all_to_all x1, blocking collectives, exchange(): return lax.all_to_all(x, 'shard', 0, 0, tiled=True)  19.4 us
    ppermute x9, starting transfers between devices, shift(): return lax.ppermute(x, 'tensor', ring)  17.4 us
    all_to_all x3, waiting for transfers between devices, exchange(): return lax.all_to_all(x, 'shard', 0, 0, tiled=True)  14.8 us
    pallas_call x2, Pallas kernels, grams(): pl.pallas_call(lambda *refs: gram_kernel(count, slot, *refs), grid=(3,),...  14.2 us
    pallas_call x2, Pallas kernels, precondition(): pl.pallas_call(lambda *refs: precond_kernel(count, shards, slot, *refs),...  12.1 us
    pallas_call x2, Pallas kernels, patch(): pl.pallas_call(lambda *refs: patch_kernel(shards, slot, *refs), grid=(1,)...  11.9 us
  transfers between devices with their start and end apart: 14, of which 5 were waited for; matrix products, arithmetic and copies ran while one was open for 0% of the time, Pallas kernels for 33%

profile of v3, /device:TPU:1, one launch (start us, length us, event | category | flops | bytes accessed | tf_op | source)
XLA Modules:
  0.0 173.7 jit_solution(16371776739395824263)
XLA Ops:
  0.6 3.8 %shard_map.115 = bf16[32,88,128]{2,1,0:T(8,128)(2,1)} custom-call(s32[32]{0:T(128)} %owner_ref.1, bf16[36,32,288]{2,1,0:T(8,128)(2,1)} %bitcast.16), custom_call_target="tpu_custom_call" | custom-call | bytes 1658880 | tf_op jit(solution)/shard_map/pallas_call | solution.py:120
  4.4 9.4 %all-to-all-start.2 = ((bf16[32,88,128]{2,1,0:T(8,128)(2,1)}), bf16[32,88,128]{2,1,0:T(8,128)(2,1)S(1)}, u32[]{:S(2)}, u32[]{:S(2)}) async-start(bf16[32,88,128]{2,1,0:T(8,128)(2,1)} %shard_map.115), calls=%async_computation.2 | async-start | bytes 1441792 | tf_op jit(solution)/shard_map/all_to_all | solution.py:575
  13.9 4.4 %shard_map.111 = bf16[32,88,128]{2,1,0:T(8,128)(2,1)} custom-call(s32[32]{0:T(128)} %owner_ref.1, bf16[36,32,288]{2,1,0:T(8,128)(2,1)} %bitcast.17), custom_call_target="tpu_custom_call" | custom-call | bytes 1658880 | tf_op jit(solution)/shard_map/pallas_call | solution.py:120
  18.3 9.1 %all-to-all-done.2.got_ref = bf16[32,88,128]{2,1,0:T(8,128)(2,1)S(1)} async-done(((bf16[32,88,128]{2,1,0:T(8,128)(2,1)}), bf16[32,88,128]{2,1,0:T(8,128)(2,1)S(1)}, u32[]{:S(2)}, u32[]{:S(2)}) %all-to-all-start.2) | async-done | bytes 720928 | tf_op jit(solution)/shard_map/all_to_all | solution.py:575
  27.4 0.9 copy-done.4
  28.3 4.4 %all-to-all-start = ((bf16[32,88,128]{2,1,0:T(8,128)(2,1)}), bf16[32,88,128]{2,1,0:T(8,128)(2,1)}, u32[]{:S(2)}, u32[]{:S(2)}) async-start(bf16[32,88,128]{2,1,0:T(8,128)(2,1)} %shard_map.111), calls=%async_computation | async-start | bytes 1441792 | tf_op jit(solution)/shard_map/all_to_all | solution.py:575
  32.7 0.0 copy-start.5
  32.7 1.1 copy-done.5
  33.8 0.4 turn.3.refs_0_.refs_3_.refs_2_
  34.2 2.8 %collective-permute-start.7 = (bf16[288,1152]{1,0:T(8,128)(2,1)S(1)}, bf16[288,1152]{1,0:T(8,128)(2,1)}, u32[]{:S(2)}, u32[]{:S(2)}) collective-permute-start(bf16[288,1152]{1,0:T(8,128)(2,1)S(1)} %turn.3.refs_0_.refs_3_.refs_2_), channel_id=1, source_target_pairs={{0,3},{1,0},{2,1},{3,2},{4,7},{5,4},{6,5},{7,6},{8,11},{9,8},{10,9... | collective-permute-start | bytes 1990664 | tf_op jit(solution)/shard_map/ppermute | solution.py:572
  37.0 3.6 %cut.1 = (bf16[288,1728]{1,0:T(8,128)(2,1)}, bf16[2,288,576]{2,1,0:T(8,128)(2,1)}) custom-call(bf16[2,288,1152]{2,1,0:T(8,128)(2,1)} %bitcast.11), custom_call_target="tpu_custom_call" | custom-call | bytes 5308416 | tf_op jit(solution)/shard_map/cut/pallas_call | solution.py:225
  40.6 0.4 collective-permute-start.1
  41.0 1.0 collective-permute-start
  42.1 4.1 %all-to-all-done.got_ref = bf16[32,88,128]{2,1,0:T(8,128)(2,1)} async-done(((bf16[32,88,128]{2,1,0:T(8,128)(2,1)}), bf16[32,88,128]{2,1,0:T(8,128)(2,1)}, u32[]{:S(2)}, u32[]{:S(2)}) %all-to-all-start) | async-done | bytes 720928 | tf_op jit(solution)/shard_map/all_to_all | solution.py:575
  46.2 2.4 %turn.2.refs_0_.refs_3_.refs_2_ = bf16[288,1152]{1,0:T(8,128)(2,1)} custom-call(bf16[32,88,128]{2,1,0:T(8,128)(2,1)} %all-to-all-done.got_ref), custom_call_target="tpu_custom_call" | custom-call | bytes 1802240 | tf_op jit(solution)/shard_map/turn/pallas_call | solution.py:152
  48.5 1.3 collective-permute-start.3
  49.8 1.3 collective-permute-start.6
  51.1 0.0 collective-permute-done.7.refs_5_.refs_4_
  51.1 3.5 %collective-permute-start.8 = (bf16[288,1152]{1,0:T(8,128)(2,1)}, bf16[288,1152]{1,0:T(8,128)(2,1)}, u32[]{:S(2)}, u32[]{:S(2)}) collective-permute-start(bf16[288,1152]{1,0:T(8,128)(2,1)} %collective-permute-done.7.refs_5_.refs_4_), channel_id=1, source_target_pairs={{0,3},{1,0},{2,1},{3,2},{4,7},{5,4},{6,5},{7,6},{8,11},{9,8},{10,9... | collective-permute-start | bytes 1990664 | tf_op jit(solution)/shard_map/ppermute | solution.py:572
  54.7 12.4 %collective-permute-done.1.refs_2_ = bf16[576,576]{1,0:T(8,128)(2,1)S(1)} collective-permute-done((bf16[576,576]{1,0:T(8,128)(2,1)}, bf16[576,576]{1,0:T(8,128)(2,1)S(1)}, u32[]{:S(2)}, u32[]{:S(2)}) %collective-permute-start.1) | collective-permute-done | bytes 663584 | tf_op jit(solution)/shard_map/ppermute | solution.py:572
  67.1 3.4 %collective-permute-start.2 = (bf16[288,576]{1,0:T(8,128)(2,1)S(1)}, bf16[288,576]{1,0:T(8,128)(2,1)S(1)}, u32[]{:S(2)}, u32[]{:S(2)}) collective-permute-start(bf16[288,576]{1,0:T(8,128)(2,1)S(1)} %slice.4), channel_id=1, source_target_pairs={{0,3},{1,0},{2,1},{3,2},{4,7},{5,4},{6,5},{7,6},{8,11},{9,8},{10,9... | collective-permute-start | bytes 995336 | tf_op jit(solution)/shard_map/ppermute | solution.py:572
  70.5 1.7 %copy-done.1 = f32[2,1152,288]{1,2,0:T(8,128)S(1)} copy-done((f32[2,1152,288]{1,2,0:T(8,128)S(1)}, f32[2,1152,288]{1,2,0:T(8,128)}, u32[]{:S(2)}) %copy-start.1) | copy-done | bytes 2654232
  72.2 2.6 %shard_map.112 = (f32[2,288,1152]{2,1,0:T(8,128)}, f32[8,128]{1,0:T(8,128)S(1)}) custom-call(bf16[288,1152]{1,0:T(8,128)(2,1)} %turn.2.refs_0_.refs_3_.refs_2_, f32[2,288,1152]{2,1,0:T(8,128)S(1)} %bitcast.8), custom_call_target="tpu_custom_call" | custom-call | flops 3317760 | bytes 3317760 | tf_op jit(solution)/shard_map/pallas_call | solution.py:176
  74.8 0.6 copy-done.8
  75.4 1.5 shard_map.116
  76.9 0.6 copy-done.9
  77.5 11.5 %collective-permute-done.2.refs_3_ = bf16[288,576]{1,0:T(8,128)(2,1)S(1)} collective-permute-done((bf16[288,576]{1,0:T(8,128)(2,1)S(1)}, bf16[288,576]{1,0:T(8,128)(2,1)S(1)}, u32[]{:S(2)}, u32[]{:S(2)}) %collective-permute-start.2) | collective-permute-done | bytes 331808 | tf_op jit(solution)/shard_map/ppermute | solution.py:572
  89.1 0.8 copy-done.11
  89.8 3.4 %collective-permute-start.4 = (bf16[288,1152]{1,0:T(8,128)(2,1)}, bf16[288,1152]{1,0:T(8,128)(2,1)}, u32[]{:S(2)}, u32[]{:S(2)}) collective-permute-start(bf16[288,1152]{1,0:T(8,128)(2,1)} %turn.2.refs_0_.refs_3_.refs_2_), channel_id=1, source_target_pairs={{0,3},{1,0},{2,1},{3,2},{4,7},{5,4},{6,5},{7,6},{8,11},{9,8},{10,9... | collective-permute-start | bytes 1990664 | tf_op jit(solution)/shard_map/ppermute | solution.py:572
  93.2 6.0 %shard_map.117.refs_2_ = bf16[1152,1536]{1,0:T(8,128)(2,1)} custom-call(bf16[2,288,1152]{2,1,0:T(8,128)(2,1)} %bitcast.12, bf16[288,1728]{1,0:T(8,128)(2,1)} %collective-permute-done.refs_1_, bf16[576,576]{1,0:T(8,128)(2,1)} %copy-done.10, bf16[288,576]{1,0:T(8,128)(2,1)} %copy-done.11), custom_call_target="tpu_custom_call" | custom-call | flops 382205952 | bytes 3981312 | tf_op jit(solution)/shard_map/pallas_call | solution.py:297
  99.2 0.3 collective-permute-start.5
  99.5 6.0 %shard_map.118 = bf16[32,88,128]{2,1,0:T(8,128)(2,1)} custom-call(bf16[2,288,1152]{2,1,0:T(8,128)(2,1)} %bitcast.14, f32[8,128]{1,0:T(8,128)} %copy-done.9, bf16[1152,1536]{1,0:T(8,128)(2,1)} %shard_map.117.refs_2_, bf16[288,1152]{1,0:T(8,128)(2,1)} %copy-done, bf16[288,1152]{1,0:T(8,128)(2,1)} %collective-permute-done.6.refs_4_.refs_3_, ...), custom_call_target="tpu_custom_call" | custom-call | flops 1528823808 | bytes 5308416 | tf_op jit(solution)/shard_map/pallas_call | solution.py:398
  105.5 8.1 %all-to-all-start.3 = ((bf16[32,88,128]{2,1,0:T(8,128)(2,1)}), bf16[32,88,128]{2,1,0:T(8,128)(2,1)S(1)}, u32[]{:S(2)}, u32[]{:S(2)}) async-start(bf16[32,88,128]{2,1,0:T(8,128)(2,1)} %shard_map.118), calls=%async_computation.3 | async-start | bytes 1441792 | tf_op jit(solution)/shard_map/all_to_all | solution.py:575
  113.7 6.0 %shard_map.113.refs_2_ = bf16[1152,1536]{1,0:T(8,128)(2,1)} custom-call(bf16[2,288,1152]{2,1,0:T(8,128)(2,1)} %bitcast.13, bf16[288,1728]{1,0:T(8,128)(2,1)} %collective-permute-done.refs_1_, bf16[576,576]{1,0:T(8,128)(2,1)} %copy-done.10, bf16[288,576]{1,0:T(8,128)(2,1)} %copy-done.11), custom_call_target="tpu_custom_call" | custom-call | flops 382205952 | bytes 3981312 | tf_op jit(solution)/shard_map/pallas_call | solution.py:297
  119.7 6.0 %shard_map.114 = bf16[32,88,128]{2,1,0:T(8,128)(2,1)} custom-call(bf16[2,288,1152]{2,1,0:T(8,128)(2,1)} %bitcast.15, f32[8,128]{1,0:T(8,128)} %copy-done.8, bf16[1152,1536]{1,0:T(8,128)(2,1)} %shard_map.113.refs_2_, bf16[288,1152]{1,0:T(8,128)(2,1)} %turn.2.refs_0_.refs_3_.refs_2_, bf16[288,1152]{1,0:T(8,128)(2,1)} %collective-permute-done.3.refs_4_.refs_3_, ...), custom_call_target="tpu_custom_call" | custom-call | flops 1528823808 | bytes 5308416 | tf_op jit(solution)/shard_map/pallas_call | solution.py:398
  125.7 1.5 all-to-all-done.3.back1_ref
  127.2 19.4 %all_to_all.20.back0_ref = bf16[32,88,128]{2,1,0:T(8,128)(2,1)S(1)} all-to-all(bf16[32,88,128]{2,1,0:T(8,128)(2,1)} %shard_map.114), channel_id=1, replica_groups=mesh['shard'=32,'tensor'=4] {'shard'}, dimensions={0} | all-to-all | bytes 1441792 | tf_op jit(solution)/shard_map/all_to_all | solution.py:575
  146.7 0.5 sums.1
  147.1 0.9 copy-done.2
  148.0 7.1 %shard_map.119 = (f32[2,288,1152]{2,1,0:T(8,128)}, f32[2,288,1152]{2,1,0:T(8,128)}) custom-call(f32[2,288,1152]{2,1,0:T(8,128)} %refs_0_.7, f32[2,288,1152]{2,1,0:T(8,128)} %refs_1_.3, bf16[288,1152]{1,0:T(8,128)(2,1)} %turn.2.refs_0_.refs_3_.refs_2_, bf16[288,1152]{1,0:T(8,128)(2,1)} %collective-permute-done.3.refs_4_.refs_3_, ...), custom_call_target="tpu_custom_call" | custom-call | flops 1528823808 | bytes 6635520 | tf_op jit(solution)/shard_map/pallas_call | solution.py:454
  155.1 3.3 %collective-permute-start.10 = (f32[8,128]{1,0:T(8,128)S(1)}, f32[8,128]{1,0:T(8,128)S(1)}, u32[]{:S(2)}, u32[]{:S(2)}) collective-permute-start(f32[8,128]{1,0:T(8,128)S(1)} %add.3.refs_0_), channel_id=1, source_target_pairs={{0,3},{1,2},{2,1},{3,0},{4,7},{5,6},{6,5},{7,4},{8,11},{9,10},{10,... | collective-permute-start | bytes 12296 | tf_op jit(solution)/shard_map/ppermute | solution.py:612
  158.4 7.1 %shard_map.120 = (f32[2,288,1152]{2,1,0:T(8,128)}, f32[2,288,1152]{2,1,0:T(8,128)}) custom-call(f32[2,288,1152]{2,1,0:T(8,128)} %refs_0_.7, f32[2,288,1152]{2,1,0:T(8,128)} %refs_1_.3, bf16[288,1152]{1,0:T(8,128)(2,1)} %copy-done, bf16[288,1152]{1,0:T(8,128)(2,1)} %collective-permute-done.6.refs_4_.refs_3_, ...), custom_call_target="tpu_custom_call", output_to_operand_aliasing={{0}: (6, {}), {1}: (7, {})} | custom-call | flops 1528823808 | bytes 6635520 | tf_op jit(solution)/shard_map/pallas_call | solution.py:454
  165.5 0.0 copy-start.3
  165.5 1.1 copy-done.3
  166.6 4.1 %place.1 = (f32[36,32,288]{2,1,0:T(8,128)S(1)}, f32[2,32,128]{2,1,0:T(8,128)S(1)}) custom-call(s32[32]{0:T(128)S(1)} %copy-done.7, bf16[32,88,128]{2,1,0:T(8,128)(2,1)S(1)} %copy-done.3, bf16[32,88,128]{2,1,0:T(8,128)(2,1)S(1)} %all-to-all-done.3.back1_ref), custom_call_target="tpu_custom_call" | custom-call | bytes 2654208 | tf_op jit(solution)/shard_map/place/pallas_call | solution.py:524
  170.7 0.0 copy-start.6
  170.7 1.5 copy-done.6
  172.2 1.5 final.1
  (23 shorter events, 0.1 us)
Async XLA Ops:
  4.4 23.0 %all-to-all-start.2 = ((bf16[32,88,128]{2,1,0:T(8,128)(2,1)}), bf16[32,88,128]{2,1,0:T(8,128)(2,1)S(1)}, u32[]{:S(2)}, u32[]{:S(2)}) async-start(bf16[32,88,128]{2,1,0:T(8,128)(2,1)} %shard_map.115), calls=%async_computation.2 | async-start | bytes 1441792 | tf_op jit(solution)/shard_map/all_to_all | solution.py:575
  27.4 0.9 copy-start.4
  28.3 17.9 %all-to-all-start = ((bf16[32,88,128]{2,1,0:T(8,128)(2,1)}), bf16[32,88,128]{2,1,0:T(8,128)(2,1)}, u32[]{:S(2)}, u32[]{:S(2)}) async-start(bf16[32,88,128]{2,1,0:T(8,128)(2,1)} %shard_map.111), calls=%async_computation | async-start | bytes 1441792 | tf_op jit(solution)/shard_map/all_to_all | solution.py:575
  32.7 1.1 copy-start.5
  34.2 41.2 %copy-start = (bf16[288,1152]{1,0:T(8,128)(2,1)}, bf16[288,1152]{1,0:T(8,128)(2,1)S(1)}, u32[]{:S(2)}) copy-start(bf16[288,1152]{1,0:T(8,128)(2,1)S(1)} %turn.3.refs_0_.refs_3_.refs_2_) | copy-start | bytes 1990660
  34.2 16.9 %collective-permute-start.7 = (bf16[288,1152]{1,0:T(8,128)(2,1)S(1)}, bf16[288,1152]{1,0:T(8,128)(2,1)}, u32[]{:S(2)}, u32[]{:S(2)}) collective-permute-start(bf16[288,1152]{1,0:T(8,128)(2,1)S(1)} %turn.3.refs_0_.refs_3_.refs_2_), channel_id=1, source_target_pairs={{0,3},{1,0},{2,1},{3,2},{4,7},{5,4},{6,5},{7,6},{8,11},{9,8},{10,9... | collective-permute-start | bytes 1990664 | tf_op jit(solution)/shard_map/ppermute | solution.py:572
  40.6 26.5 %collective-permute-start.1 = (bf16[576,576]{1,0:T(8,128)(2,1)}, bf16[576,576]{1,0:T(8,128)(2,1)S(1)}, u32[]{:S(2)}, u32[]{:S(2)}) collective-permute-start(bf16[576,576]{1,0:T(8,128)(2,1)} %bitcast.20), channel_id=1, source_target_pairs={{0,3},{1,0},{2,1},{3,2},{4,7},{5,4},{6,5},{7,6},{8,11},{9,8},{10,9... | collective-permute-start | bytes 1990664 | tf_op jit(solution)/shard_map/ppermute | solution.py:572
  41.0 52.2 %collective-permute-start = (bf16[288,1728]{1,0:T(8,128)(2,1)}, bf16[288,1728]{1,0:T(8,128)(2,1)}, u32[]{:S(2)}, u32[]{:S(2)}) collective-permute-start(bf16[288,1728]{1,0:T(8,128)(2,1)} %get-tuple-element.17), channel_id=1, source_target_pairs={{0,1},{1,2},{2,3},{3,0},{4,5},{5,6},{6,7},{7,4},{8,9},{9,10},{10,1... | collective-permute-start | bytes 2985992 | tf_op jit(solution)/shard_map/ppermute | solution.py:572
  48.5 50.7 %collective-permute-start.3 = (bf16[288,1152]{1,0:T(8,128)(2,1)}, bf16[288,1152]{1,0:T(8,128)(2,1)}, u32[]{:S(2)}, u32[]{:S(2)}) collective-permute-start(bf16[288,1152]{1,0:T(8,128)(2,1)} %turn.2.refs_0_.refs_3_.refs_2_), channel_id=1, source_target_pairs={{0,1},{1,2},{2,3},{3,0},{4,5},{5,6},{6,7},{7,4},{8,9},{9,10},{10,1... | collective-permute-start | bytes 1990664 | tf_op jit(solution)/shard_map/ppermute | solution.py:572
  49.8 49.6 %collective-permute-start.6 = (bf16[288,1152]{1,0:T(8,128)(2,1)S(1)}, bf16[288,1152]{1,0:T(8,128)(2,1)}, u32[]{:S(2)}, u32[]{:S(2)}) collective-permute-start(bf16[288,1152]{1,0:T(8,128)(2,1)S(1)} %turn.3.refs_0_.refs_3_.refs_2_), channel_id=1, source_target_pairs={{0,1},{1,2},{2,3},{3,0},{4,5},{5,6},{6,7},{7,4},{8,9},{9,10},{10,1... | collective-permute-start | bytes 1990664 | tf_op jit(solution)/shard_map/ppermute | solution.py:572
  51.1 48.3 %collective-permute-start.8 = (bf16[288,1152]{1,0:T(8,128)(2,1)}, bf16[288,1152]{1,0:T(8,128)(2,1)}, u32[]{:S(2)}, u32[]{:S(2)}) collective-permute-start(bf16[288,1152]{1,0:T(8,128)(2,1)} %collective-permute-done.7.refs_5_.refs_4_), channel_id=1, source_target_pairs={{0,3},{1,0},{2,1},{3,2},{4,7},{5,4},{6,5},{7,6},{8,11},{9,8},{10,9... | collective-permute-start | bytes 1990664 | tf_op jit(solution)/shard_map/ppermute | solution.py:572
  67.1 9.9 %copy-start.10 = (bf16[576,576]{1,0:T(8,128)(2,1)}, bf16[576,576]{1,0:T(8,128)(2,1)S(1)}, u32[]{:S(2)}) copy-start(bf16[576,576]{1,0:T(8,128)(2,1)S(1)} %collective-permute-done.1.refs_2_) | copy-start | bytes 1990660
  67.1 22.0 %collective-permute-start.2 = (bf16[288,576]{1,0:T(8,128)(2,1)S(1)}, bf16[288,576]{1,0:T(8,128)(2,1)S(1)}, u32[]{:S(2)}, u32[]{:S(2)}) collective-permute-start(bf16[288,576]{1,0:T(8,128)(2,1)S(1)} %slice.4), channel_id=1, source_target_pairs={{0,3},{1,0},{2,1},{3,2},{4,7},{5,4},{6,5},{7,6},{8,11},{9,8},{10,9... | collective-permute-start | bytes 995336 | tf_op jit(solution)/shard_map/ppermute | solution.py:572
  70.5 1.7 %copy-start.1 = (f32[2,1152,288]{1,2,0:T(8,128)S(1)}, f32[2,1152,288]{1,2,0:T(8,128)}, u32[]{:S(2)}) copy-start(f32[2,1152,288]{1,2,0:T(8,128)} %param.15) | copy-start | bytes 7962628
  74.8 0.6 copy-start.8
  76.9 0.6 copy-start.9
  89.1 0.8 copy-start.11
  89.8 29.8 %collective-permute-start.4 = (bf16[288,1152]{1,0:T(8,128)(2,1)}, bf16[288,1152]{1,0:T(8,128)(2,1)}, u32[]{:S(2)}, u32[]{:S(2)}) collective-permute-start(bf16[288,1152]{1,0:T(8,128)(2,1)} %turn.2.refs_0_.refs_3_.refs_2_), channel_id=1, source_target_pairs={{0,3},{1,0},{2,1},{3,2},{4,7},{5,4},{6,5},{7,6},{8,11},{9,8},{10,9... | collective-permute-start | bytes 1990664 | tf_op jit(solution)/shard_map/ppermute | solution.py:572
  99.2 20.4 %collective-permute-start.5 = (bf16[288,1152]{1,0:T(8,128)(2,1)}, bf16[288,1152]{1,0:T(8,128)(2,1)}, u32[]{:S(2)}, u32[]{:S(2)}) collective-permute-start(bf16[288,1152]{1,0:T(8,128)(2,1)} %collective-permute-done.3.refs_4_.refs_3_), channel_id=1, source_target_pairs={{0,1},{1,2},{2,3},{3,0},{4,5},{5,6},{6,7},{7,4},{8,9},{9,10},{10,1... | collective-permute-start | bytes 1990664 | tf_op jit(solution)/shard_map/ppermute | solution.py:572
  105.5 21.7 %all-to-all-start.3 = ((bf16[32,88,128]{2,1,0:T(8,128)(2,1)}), bf16[32,88,128]{2,1,0:T(8,128)(2,1)S(1)}, u32[]{:S(2)}, u32[]{:S(2)}) async-start(bf16[32,88,128]{2,1,0:T(8,128)(2,1)} %shard_map.118), calls=%async_computation.3 | async-start | bytes 1441792 | tf_op jit(solution)/shard_map/all_to_all | solution.py:575
  147.1 0.9 copy-start.2
  148.0 7.1 %collective-permute-start.9 = (f32[8,128]{1,0:T(8,128)S(1)}, f32[8,128]{1,0:T(8,128)S(1)}, u32[]{:S(2)}, u32[]{:S(2)}) collective-permute-start(f32[8,128]{1,0:T(8,128)S(1)} %sums.1), channel_id=1, source_target_pairs={{0,1},{1,0},{2,3},{3,2},{4,5},{5,4},{6,7},{7,6},{8,9},{9,8},{10,11... | collective-permute-start | bytes 12296 | tf_op jit(solution)/shard_map/ppermute | solution.py:612
  155.1 15.6 %collective-permute-start.10 = (f32[8,128]{1,0:T(8,128)S(1)}, f32[8,128]{1,0:T(8,128)S(1)}, u32[]{:S(2)}, u32[]{:S(2)}) collective-permute-start(f32[8,128]{1,0:T(8,128)S(1)} %add.3.refs_0_), channel_id=1, source_target_pairs={{0,3},{1,2},{2,1},{3,0},{4,7},{5,6},{6,5},{7,4},{8,11},{9,10},{10,... | collective-permute-start | bytes 12296 | tf_op jit(solution)/shard_map/ppermute | solution.py:612
  158.4 7.1 %copy-start.7 = (s32[32]{0:T(128)S(1)}, s32[32]{0:T(128)}, u32[]{:S(2)}) copy-start(s32[32]{0:T(128)} %owner_ref.1) | copy-start | bytes 388
  165.5 1.1 copy-start.3
  170.7 1.5 copy-start.6
